TPU v7x, 256 devices: a whole 4x4x8 slice. The times are simulated.
256 devices in a mesh: gx: 2 (over z_hi), gy: 16 (over x, y), grp: 8 (over z_lo, core).
Axes of the slice: x: 4, y: 4, z: 8 (z_hi: 2, z_lo: 4; z = z_hi * 4 + z_lo), core: 2. Of those that a mesh axis runs over, the one named last changes fastest.
Arguments:
- field_in: bfloat16 [8, 16, 256, 1024], P('grp', 'gx', 'gy'), may hold values from -6 to 6
- first_weight: bfloat16 [3, 3, 3, 64, 64], replicated, may hold values from -0.15625 to 0.15625
- second_weight: bfloat16 [3, 3, 3, 64, 64], replicated, may hold values from -0.15625 to 0.15625
- cotangent: bfloat16 [8, 16, 256, 1024], P('grp', 'gx', 'gy'), may hold values from -6 to 6
Outputs:
- field_out: bfloat16 [8, 16, 256, 1024], P('grp', 'gx', 'gy')
- first_grad: float32 [3, 3, 3, 64, 64], replicated
- second_grad: float32 [3, 3, 3, 64, 64], replicated
All inputs are finite; a program needn't handle non-finite values.
Results may differ from a plain program's by a relative error of at most 0.0095.
Values may be sent and summed in bfloat16 or wider, within the bound.
A program may use at most 64 MiB of HBM per device.

v0:
```python
import math

import jax
import jax.numpy as jnp
from jax import lax
from jax.sharding import PartitionSpec as P

C = 64
NZ = 16


def extended(cells, sides, width):
    for axis, dim in sides:
        count = lax.axis_size(axis)
        ends = count - 1
        head = lax.slice_in_dim(cells, 0, width, axis=dim)
        tail = lax.slice_in_dim(cells, cells.shape[dim] - width, cells.shape[dim], axis=dim)
        cells = jnp.concatenate(
            [
                lax.ppermute(tail, axis, [(i, (i + 1) % count) for i in range(ends)]),
                cells,
                lax.ppermute(head, axis, [((i + 1) % count, i) for i in range(ends)]),
            ],
            axis=dim,
        )
    return cells


def conv_local(padded, weight):
    return lax.conv_general_dilated(
        padded,
        weight,
        (1, 1, 1),
        ((0, 0), (0, 0), (1, 1)),
        dimension_numbers=("NHWDC", "HWDIO", "NHWDC"),
        preferred_element_type=jnp.float32,
    )


def kernel_local(padded, grad_out):
    result = lax.conv_general_dilated(
        padded,
        grad_out,
        (1, 1, 1),
        ((0, 0), (0, 0), (1, 1)),
        dimension_numbers=("CHWDN", "IHWDO", "NHWDC"),
        preferred_element_type=jnp.float32,
    )
    return jnp.transpose(result, (1, 2, 3, 0, 4))


def as_cells(field):
    return field.reshape(field.shape[0], field.shape[1], field.shape[2], NZ, C)


def reduce_grad(local):
    return lax.psum(local, ("gx", "gy", "grp"))


def shards(field_in, first_weight, second_weight, cotangent):
    total = (
        field_in.shape[0]
        * field_in.shape[1]
        * field_in.shape[2]
        * NZ
        * lax.axis_size("gx")
        * lax.axis_size("gy")
        * lax.axis_size("grp")
    )
    factor = 1.0 / math.sqrt(total)
    padded_in = extended(field_in, (("gx", 1), ("gy", 2)), 1)
    pre_first = conv_local(as_cells(padded_in), first_weight)
    hidden = jax.nn.silu(pre_first).astype(jnp.bfloat16)
    flat_hidden = hidden.reshape(field_in.shape)
    padded_hidden = extended(flat_hidden, (("gx", 1), ("gy", 2)), 1)
    output = conv_local(as_cells(padded_hidden), second_weight).astype(jnp.bfloat16)
    padded_grad = extended(cotangent, (("gx", 1), ("gy", 2)), 1)
    grad_cells = as_cells(cotangent)
    second_local = kernel_local(as_cells(padded_hidden), grad_cells) * factor
    second_grad = reduce_grad(second_local)
    flipped = jnp.swapaxes(second_weight[::-1, ::-1, ::-1], 3, 4)
    hidden_grad = conv_local(as_cells(padded_grad), flipped)
    sigma = jax.nn.sigmoid(pre_first)
    pre_grad = (hidden_grad * sigma * (1.0 + pre_first * (1.0 - sigma))).astype(jnp.bfloat16)
    first_local = kernel_local(as_cells(padded_in), pre_grad) * factor
    first_grad = reduce_grad(first_local)
    return (output.reshape(field_in.shape), first_grad, second_grad)


def solution(mesh):
    return jax.shard_map(
        shards,
        mesh=mesh,
        in_specs=(P("grp", "gx", "gy", None), P(), P(), P("grp", "gx", "gy", None)),
        out_specs=(P("grp", "gx", "gy", None), P(), P()),
        check_vma=False,
    )
```

profile of v0, /device:TPU:1, one launch (start us, length us, event | category | flops | bytes accessed | tf_op | source)
XLA Modules:
  0.0 418.3 jit_solution(2581174802621383677)
XLA Ops:
  7.2 0.8 fusion.84
  8.1 9.6 %collective-permute-start = (bf16[1,1,16,1024]{3,2,1,0:T(8,128)(2,1)S(1)}, bf16[1,1,16,1024]{3,2,1,0:T(8,128)(2,1)S(1)}, u32[]{:S(2)}, u32[]{:S(2)}) collective-permute-start(bf16[1,1,16,1024]{3,2,1,0:T(8,128)(2,1)S(1)} %get-tuple-element.22), channel_id=1, source_target_pairs={{0,128},{1,129},{2,130},{3,131},{4,132},{5,133},{6,134},{7,135},{8... | collective-permute-start | bytes 98312 | tf_op jit(solution)/shard_map/ppermute | solution.py:20
  17.7 1.3 collective-permute-start.1
  19.0 0.8 fusion.82
  19.8 7.9 %collective-permute-start.8 = (bf16[1,1,16,1024]{3,2,1,0:T(8,128)(2,1)S(1)}, bf16[1,1,16,1024]{3,2,1,0:T(8,128)(2,1)S(1)}, u32[]{:S(2)}, u32[]{:S(2)}) collective-permute-start(bf16[1,1,16,1024]{3,2,1,0:T(8,128)(2,1)S(1)} %get-tuple-element.18), channel_id=1, source_target_pairs={{0,128},{1,129},{2,130},{3,131},{4,132},{5,133},{6,134},{7,135},{8... | collective-permute-start | bytes 98312 | tf_op jit(solution)/shard_map/ppermute | solution.py:20
  27.7 1.3 collective-permute-start.9
  29.0 3.5 reshape.92
  32.6 1.3 collective-permute-start.3
  33.9 4.0 collective-permute-start.2
  38.0 0.8 fusion.79
  38.8 1.3 collective-permute-start.11
  40.1 4.6 %collective-permute-start.10 = (bf16[1,10,1,1024]{3,2,1,0:T(2,128)(2,1)}, bf16[1,10,1,1024]{3,2,1,0:T(2,128)(2,1)}, u32[]{:S(2)}, u32[]{:S(2)}) collective-permute-start(bf16[1,10,1,1024]{3,2,1,0:T(2,128)(2,1)} %get-tuple-element.11), channel_id=1, source_target_pairs={{0,8},{8,16},{16,24},{24,32},{32,40},{40,48},{48,56},{56,64},{64,7... | collective-permute-start | bytes 61448 | tf_op jit(solution)/shard_map/ppermute | solution.py:20
  44.7 0.2 pad_maximum_fusion
  44.9 0.5 reshape.65
  45.4 1.5 fusion.78
  46.9 0.7 reshape.54
  47.6 2.2 fusion.77
  49.7 2.1 fusion.76
  51.9 2.8 reshape.34
  54.7 0.2 copy.27
  54.9 0.2 slice.59
  55.1 0.2 copy-done.17
  55.4 4.3 %multiply_convert_fusion.1 = (bf16[8,16,8,3,64]{4,2,3,1,0:T(8,128)(2,1)S(1)}, f32[8,16,8,3,64]{4,2,3,1,0:T(8,128)}) fusion(pred[8,3]{0,1:T(4,128)(4,1)S(1)} %copy-done.17, bf16[3,3,3,64,64]{4,3,2,1,0:T(8,128)(2,1)S(1)} %copy-done, bf16[10,18,1,7,2,64]{5,3,4,1,0,2:T(8,128)(2,1)S(1)} %slice.59, bf16[10,18,1,8,3,64]{5,3,4,1,0,2:T(8,128)(2,1)S(1)} %copy.27), kind=kOutput, calls=%fused_computation.34 | convolution fusion | flops 683421696 | bytes 2276376 | tf_op jit(solution)/shard_map/conv_general_dilated | solution.py:30
  59.6 0.1 copy.28
  59.8 0.1 copy.29
  60.0 1.1 reshape.27
  61.0 1.4 fusion.83
  62.4 8.5 %collective-permute-start.4 = (bf16[1,1,16,1024]{3,2,1,0:T(8,128)(2,1)}, bf16[1,1,16,1024]{3,2,1,0:T(8,128)(2,1)}, u32[]{:S(2)}, u32[]{:S(2)}) collective-permute-start(bf16[1,1,16,1024]{3,2,1,0:T(8,128)(2,1)} %get-tuple-element.20), channel_id=1, source_target_pairs={{0,128},{1,129},{2,130},{3,131},{4,132},{5,133},{6,134},{7,135},{8... | collective-permute-start | bytes 98312 | tf_op jit(solution)/shard_map/ppermute | solution.py:20
  70.9 1.5 collective-permute-start.5
  72.5 1.2 copy.47
  73.7 0.1 copy.46
  73.9 0.8 copy-done.5
  74.8 1.9 fusion.49
  76.7 1.0 pad_maximum_fusion.2
  77.7 0.7 reshape.59
  78.4 1.2 copy.38
  79.6 0.5 reshape.84
  80.1 0.4 pad.4
  80.5 0.7 reshape.48
  81.2 0.2 copy.40
  81.4 0.2 slice.73
  81.6 0.9 constant_dynamic-update-slice_fusion.5
  82.6 0.7 copy-done.12
  83.4 1.3 collective-permute-start.7
  84.7 4.0 collective-permute-start.6
  88.7 27.1 %fusion.39 = f32[3,3,3,64,64]{4,3,2,1,0:T(8,128)} fusion(bf16[10,18,8,3,64,1]{4,2,5,3,1,0:T(8,128)(2,1)} %get-tuple-element.25, bf16[10,18,8,3,64,1]{4,2,5,3,1,0:T(8,128)(2,1)S(1)} %copy-done.9, bf16[10,18,8,3,64,1]{4,2,5,3,1,0:T(8,128)(2,1)} %get-tuple-element.26, f32[8,16,8,3,64]{4,2,3,1,0:T(8,128)} %get-tuple-element.24, ...), kind=kOutput, calls=%fused_computation.38 | convolution fusion | flops 1365848064 | bytes 3984408 | tf_op jit(solution)/shard_map/transpose | solution.py:49
  115.8 1.2 pad_maximum_fusion.1
  117.0 0.5 reshape.71
  117.5 2.7 reshape.91
  120.2 0.4 pad.2
  120.6 0.7 reshape.41
  121.3 0.2 copy.31
  121.5 1.0 copy-done.1
  122.5 1.0 slice.65
  123.6 13.9 %convolution_multiply_fusion = f32[3,3,3,64,64]{4,3,2,1,0:T(8,128)} fusion(bf16[1,10,18,16,64]{4,0,3,2,1:T(2,128)(2,1)S(1)} %copy-done.6, bf16[1,8,16,16,64]{4,0,3,2,1:T(2,128)(2,1)S(1)} %copy-done.10), kind=kOutput, calls=%fused_computation.37 | convolution fusion | flops 434221056 | bytes 1073152 | tf_op jit(solution)/shard_map/transpose | solution.py:49
  137.7 1.0 copy-done.2
  138.7 0.1 copy-done.16
  138.8 4.2 %select_convert_fusion = bf16[8,16,8,3,64]{4,2,3,1,0:T(8,128)(2,1)S(1)} fusion(bf16[3,3,3,64,64]{4,3,2,1,0:T(8,128)(2,1)S(1)} %copy-done.16, bf16[10,18,1,7,2,64]{5,3,4,1,0,2:T(8,128)(2,1)} %slice.65, bf16[10,18,1,8,3,64]{5,3,4,1,0,2:T(8,128)(2,1)S(1)} %copy-done.2, pred[8,3]{0,1:T(4,128)(4,1)S(1)} %copy-done.18), kind=kOutput, calls=%fused_computation.33 | convolution fusion | flops 682635264 | bytes 1489944 | tf_op jit(solution)/shard_map/conv_general_dilated | solution.py:30
  143.0 0.1 copy.32
  143.2 0.1 copy.33
  143.4 1.1 reshape.29
  144.4 263.7 %all-reduce.3.cloned.1.call-done = (f32[3,3,3,64,64]{4,3,2,1,0:T(8,128)}, f32[3,3,3,64,64]{4,3,2,1,0:T(8,128)}) async-done(((f32[3,3,3,64,64]{4,3,2,1,0:T(8,128)}, f32[3,3,3,64,64]{4,3,2,1,0:T(8,128)}), (f32[3,3,3,64,64]{4,3,2,1,0:T(8,128)}, f32[3,3,3,64,64]{4,3,2,1,0:T(8,128)})) %all-reduce.3.cloned.1.call-update) | async-done | bytes 884752 | tf_op jit(solution)/shard_map/psum | solution.py:57
  408.1 2.3 copy.56
  410.3 0.9 copy.57
  (60 shorter events, 0.6 us)
Async XLA Ops:
  7.2 48.0 %copy-start = (bf16[3,3,3,64,64]{4,3,2,1,0:T(8,128)(2,1)S(1)}, bf16[3,3,3,64,64]{4,3,2,1,0:T(8,128)(2,1)}, u32[]{:S(2)}) copy-start(bf16[3,3,3,64,64]{4,3,2,1,0:T(8,128)(2,1)} %param.5) | copy-start | bytes 663556
  7.2 25.3 %copy-start.15 = (bf16[1,8,16,1024]{3,2,1,0:T(8,128)(2,1)S(1)}, bf16[1,8,16,1024]{3,2,1,0:T(8,128)(2,1)}, u32[]{:S(2)}) copy-start(bf16[1,8,16,1024]{3,2,1,0:T(8,128)(2,1)} %param.4) | copy-start | bytes 786436
  7.2 30.8 %copy-start.7 = (bf16[1,8,16,1024]{3,2,1,0:T(8,128)(2,1)S(1)}, bf16[1,8,16,1024]{3,2,1,0:T(8,128)(2,1)}, u32[]{:S(2)}) copy-start(bf16[1,8,16,1024]{3,2,1,0:T(8,128)(2,1)} %param.7) | copy-start | bytes 786436
  7.2 400.9 %all-reduce.3.cloned.1.call-start = ((), (), s32[]{:S(2)}) async-start(), calls=%async_computation | async-start | bytes 3538944 | tf_op jit(solution)/shard_map/psum | solution.py:57
  8.1 24.4 %collective-permute-start = (bf16[1,1,16,1024]{3,2,1,0:T(8,128)(2,1)S(1)}, bf16[1,1,16,1024]{3,2,1,0:T(8,128)(2,1)S(1)}, u32[]{:S(2)}, u32[]{:S(2)}) collective-permute-start(bf16[1,1,16,1024]{3,2,1,0:T(8,128)(2,1)S(1)} %get-tuple-element.22), channel_id=1, source_target_pairs={{0,128},{1,129},{2,130},{3,131},{4,132},{5,133},{6,134},{7,135},{8... | collective-permute-start | bytes 98312 | tf_op jit(solution)/shard_map/ppermute | solution.py:20
  17.7 14.8 %collective-permute-start.1 = (bf16[1,1,16,1024]{3,2,1,0:T(8,128)(2,1)S(1)}, bf16[1,1,16,1024]{3,2,1,0:T(8,128)(2,1)S(1)}, u32[]{:S(2)}, u32[]{:S(2)}) collective-permute-start(bf16[1,1,16,1024]{3,2,1,0:T(8,128)(2,1)S(1)} %get-tuple-element.21), channel_id=1, source_target_pairs={{128,0},{129,1},{130,2},{131,3},{132,4},{133,5},{134,6},{135,7},{1... | collective-permute-start | bytes 98312 | tf_op jit(solution)/shard_map/ppermute | solution.py:22
  19.8 18.1 %collective-permute-start.8 = (bf16[1,1,16,1024]{3,2,1,0:T(8,128)(2,1)S(1)}, bf16[1,1,16,1024]{3,2,1,0:T(8,128)(2,1)S(1)}, u32[]{:S(2)}, u32[]{:S(2)}) collective-permute-start(bf16[1,1,16,1024]{3,2,1,0:T(8,128)(2,1)S(1)} %get-tuple-element.18), channel_id=1, source_target_pairs={{0,128},{1,129},{2,130},{3,131},{4,132},{5,133},{6,134},{7,135},{8... | collective-permute-start | bytes 98312 | tf_op jit(solution)/shard_map/ppermute | solution.py:20
  27.7 10.3 %collective-permute-start.9 = (bf16[1,1,16,1024]{3,2,1,0:T(8,128)(2,1)S(1)}, bf16[1,1,16,1024]{3,2,1,0:T(8,128)(2,1)S(1)}, u32[]{:S(2)}, u32[]{:S(2)}) collective-permute-start(bf16[1,1,16,1024]{3,2,1,0:T(8,128)(2,1)S(1)} %get-tuple-element.17), channel_id=1, source_target_pairs={{128,0},{129,1},{130,2},{131,3},{132,4},{133,5},{134,6},{135,7},{1... | collective-permute-start | bytes 98312 | tf_op jit(solution)/shard_map/ppermute | solution.py:22
  32.6 12.0 %collective-permute-start.3 = (bf16[1,10,1,1024]{3,2,1,0:T(2,128)(2,1)S(1)}, bf16[1,10,1,1024]{3,2,1,0:T(2,128)(2,1)S(1)}, u32[]{:S(2)}, u32[]{:S(2)}) collective-permute-start(bf16[1,10,1,1024]{3,2,1,0:T(2,128)(2,1)S(1)} %get-tuple-element.16), channel_id=1, source_target_pairs={{8,0},{16,8},{24,16},{32,24},{40,32},{48,40},{56,48},{64,56},{72,6... | collective-permute-start | bytes 61448 | tf_op jit(solution)/shard_map/ppermute | solution.py:22
  33.9 10.7 %collective-permute-start.2 = (bf16[1,10,1,1024]{3,2,1,0:T(2,128)(2,1)S(1)}, bf16[1,10,1,1024]{3,2,1,0:T(2,128)(2,1)S(1)}, u32[]{:S(2)}, u32[]{:S(2)}) collective-permute-start(bf16[1,10,1,1024]{3,2,1,0:T(2,128)(2,1)S(1)} %get-tuple-element.15), channel_id=1, source_target_pairs={{0,8},{8,16},{16,24},{24,32},{32,40},{40,48},{48,56},{56,64},{64,7... | collective-permute-start | bytes 61448 | tf_op jit(solution)/shard_map/ppermute | solution.py:20
  38.0 6.7 %copy-start.13 = (bf16[1,10,16,1024]{3,2,1,0:T(8,128)(2,1)}, bf16[1,10,16,1024]{3,2,1,0:T(8,128)(2,1)S(1)}, u32[]{:S(2)}) copy-start(bf16[1,10,16,1024]{3,2,1,0:T(8,128)(2,1)S(1)} %constant_dynamic-update-slice_fusion.6) | copy-start | bytes 983044
  38.8 37.9 %collective-permute-start.11 = (bf16[1,10,1,1024]{3,2,1,0:T(2,128)(2,1)}, bf16[1,10,1,1024]{3,2,1,0:T(2,128)(2,1)}, u32[]{:S(2)}, u32[]{:S(2)}) collective-permute-start(bf16[1,10,1,1024]{3,2,1,0:T(2,128)(2,1)} %get-tuple-element.12), channel_id=1, source_target_pairs={{8,0},{16,8},{24,16},{32,24},{40,32},{48,40},{56,48},{64,56},{72,6... | collective-permute-start | bytes 61448 | tf_op jit(solution)/shard_map/ppermute | solution.py:22
  40.1 36.6 %collective-permute-start.10 = (bf16[1,10,1,1024]{3,2,1,0:T(2,128)(2,1)}, bf16[1,10,1,1024]{3,2,1,0:T(2,128)(2,1)}, u32[]{:S(2)}, u32[]{:S(2)}) collective-permute-start(bf16[1,10,1,1024]{3,2,1,0:T(2,128)(2,1)} %get-tuple-element.11), channel_id=1, source_target_pairs={{0,8},{8,16},{16,24},{24,32},{32,40},{40,48},{48,56},{56,64},{64,7... | collective-permute-start | bytes 61448 | tf_op jit(solution)/shard_map/ppermute | solution.py:20
  54.7 0.7 copy-start.17
  59.8 13.8 %copy-start.4 = (bf16[10,18,1,8,2,64]{5,4,3,1,0,2:T(2,128)(2,1)S(1)}, bf16[10,18,1,8,2,64]{5,4,3,1,0,2:T(2,128)(2,1)}, u32[]{:S(2)}) copy-start(bf16[10,18,1,8,2,64]{5,4,3,1,0,2:T(2,128)(2,1)} %get-tuple-element.6) | copy-start | bytes 1105924
  60.0 13.8 %copy-start.3 = (bf16[10,18,1,8,2,64]{5,4,3,1,0,2:T(2,128)(2,1)S(1)}, bf16[10,18,1,8,2,64]{5,4,3,1,0,2:T(2,128)(2,1)}, u32[]{:S(2)}) copy-start(bf16[10,18,1,8,2,64]{5,4,3,1,0,2:T(2,128)(2,1)} %get-tuple-element.5) | copy-start | bytes 1105924
  62.4 19.2 %collective-permute-start.4 = (bf16[1,1,16,1024]{3,2,1,0:T(8,128)(2,1)}, bf16[1,1,16,1024]{3,2,1,0:T(8,128)(2,1)}, u32[]{:S(2)}, u32[]{:S(2)}) collective-permute-start(bf16[1,1,16,1024]{3,2,1,0:T(8,128)(2,1)} %get-tuple-element.20), channel_id=1, source_target_pairs={{0,128},{1,129},{2,130},{3,131},{4,132},{5,133},{6,134},{7,135},{8... | collective-permute-start | bytes 98312 | tf_op jit(solution)/shard_map/ppermute | solution.py:20
  70.9 11.6 %collective-permute-start.5 = (bf16[1,1,16,1024]{3,2,1,0:T(8,128)(2,1)}, bf16[1,1,16,1024]{3,2,1,0:T(8,128)(2,1)S(1)}, u32[]{:S(2)}, u32[]{:S(2)}) collective-permute-start(bf16[1,1,16,1024]{3,2,1,0:T(8,128)(2,1)} %get-tuple-element.19), channel_id=1, source_target_pairs={{128,0},{129,1},{130,2},{131,3},{132,4},{133,5},{134,6},{135,7},{1... | collective-permute-start | bytes 98312 | tf_op jit(solution)/shard_map/ppermute | solution.py:22
  73.6 1.1 copy-start.5
  74.8 1.9 copy-start.14
  81.2 1.3 copy-start.8
  81.4 7.2 %copy-start.9 = (bf16[10,18,8,3,64,1]{4,2,5,3,1,0:T(8,128)(2,1)S(1)}, bf16[10,18,8,3,64,1]{4,2,5,3,1,0:T(8,128)(2,1)}, u32[]{:S(2)}) copy-start(bf16[10,18,8,3,64,1]{4,2,5,3,1,0:T(8,128)(2,1)} %copy.38) | copy-start | bytes 1658884
  82.6 0.7 copy-start.12
  83.4 32.5 %collective-permute-start.7 = (bf16[1,10,1,1024]{3,2,1,0:T(2,128)(2,1)S(1)}, bf16[1,10,1,1024]{3,2,1,0:T(2,128)(2,1)S(1)}, u32[]{:S(2)}, u32[]{:S(2)}) collective-permute-start(bf16[1,10,1,1024]{3,2,1,0:T(2,128)(2,1)S(1)} %get-tuple-element.14), channel_id=1, source_target_pairs={{8,0},{16,8},{24,16},{32,24},{40,32},{48,40},{56,48},{64,56},{72,6... | collective-permute-start | bytes 61448 | tf_op jit(solution)/shard_map/ppermute | solution.py:22
  84.7 31.2 %collective-permute-start.6 = (bf16[1,10,1,1024]{3,2,1,0:T(2,128)(2,1)S(1)}, bf16[1,10,1,1024]{3,2,1,0:T(2,128)(2,1)S(1)}, u32[]{:S(2)}, u32[]{:S(2)}) collective-permute-start(bf16[1,10,1,1024]{3,2,1,0:T(2,128)(2,1)S(1)} %get-tuple-element.13), channel_id=1, source_target_pairs={{0,8},{8,16},{16,24},{24,32},{32,40},{40,48},{48,56},{56,64},{64,7... | collective-permute-start | bytes 61448 | tf_op jit(solution)/shard_map/ppermute | solution.py:20
  121.3 2.3 copy-start.6
  121.3 2.3 copy-start.10
  121.5 1.0 copy-start.1
  137.5 1.2 copy-start.2
  137.5 1.3 copy-start.16
  137.5 1.3 copy-start.18
  408.1 2.3 copy-start.11
Sparse Core Ops, SparseCore 0:
  137.8 270.1 all-reduce.2
where the time goes:
time: 422 us; the launch traced here: 418 us
  waiting for transfers between devices  264 us (63%)
  matrix products  49.5 us (12%)
  starting transfers between devices  46.6 us (11%)
  local copies, waits for them, and re-layouts  39.2 us (9%)
  between operations  15 us (4%)
  other arithmetic  4.27 us (1%)
    psum x1, waiting for transfers between devices, reduce_grad(): return lax.psum(local, ('gx', 'gy', 'grp'))  264 us
    transpose x2, matrix products, kernel_local(): return jnp.transpose(result, (1, 2, 3, 0, 4))  41.1 us
    ppermute x6, starting transfers between devices, extended(): lax.ppermute(tail, axis, [(i, (i + 1) % count) for i in range(ends)])  38.6 us
    reshape x13, local copies, waits for them, and re-layouts, as_cells(): return field.reshape(field.shape[0], field.shape[1], field.shape[2], NZ, C)  16.8 us
    unnamed x50, local copies, waits for them, and re-layouts  9.51 us
    conv_general_dilated x2, matrix products, conv_local(): lax.conv_general_dilated(padded, weight, (1, 1, 1), ((0, 0), (0, 0), (1,...  8.46 us
  transfers between devices with their start and end apart: 13, of which 1 were waited for; matrix products, arithmetic and copies ran while one was open for 15% of the time, Pallas kernels for 0%

commit v1 on v0

v1 whole, which is shorter than its diff:
```python
import functools
import math

import jax
import jax.numpy as jnp
from jax import lax
from jax.experimental import pallas as pl
from jax.experimental.pallas import tpu as pltpu
from jax.sharding import PartitionSpec as P

C = 64
NZ = 16
X = 8
Y = 16
Q = 8
XE = X + 2
YE = Y + 2
ROWS_E = XE * Y
PAIRS = 5
PACKED = PAIRS * 192
CELLS = 2 * X + Y + 2
F32 = jnp.float32
BF16 = jnp.bfloat16
MESH = pl.DeviceIdType.MESH


def low_lanes(rows):
    return lax.broadcasted_iota(jnp.int32, (rows, 128), 1) < 64


def fill_own(ext, x, q, value):
    ext[pl.ds(((x + 1) * YE + 1) * Q + q, Y, stride=Q), :] = value


def edge_cells(ext, sends, gx):
    near = X - (X - 1) * gx
    for y in range(Y):
        start = pl.multiple_of((near * YE + 1 + y) * Q, Q)
        sends[y] = ext[pl.ds(start, Q), :].astype(BF16)
    for x in range(X):
        sends[Y + x] = ext[pl.ds(((x + 1) * YE + 1) * Q, Q), :].astype(BF16)
        sends[Y + X + x] = ext[pl.ds(((x + 1) * YE + Y) * Q, Q), :].astype(BF16)


def halo_copies(sends, lands, send_sems, recv_sem, gx, gy, grp, count):
    up = lax.rem(gy + 1, count)
    down = lax.rem(gy + count - 1, count)
    other = 1 - gx
    moves = (
        (0, Y, 0, other, gy),
        (Y, X, Y + X, gx, down),
        (Y + X, X, Y, gx, up),
        (0, 1, 2 * X + Y + 1, other, down),
        (Y - 1, 1, 2 * X + Y, other, up),
    )
    for number, (source, size, target, to_x, to_y) in enumerate(moves):
        pltpu.make_async_remote_copy(
            src_ref=sends.at[pl.ds(source, size)],
            dst_ref=lands.at[pl.ds(target, size)],
            send_sem=send_sems.at[number],
            recv_sem=recv_sem,
            device_id=(to_x, to_y, grp),
            device_id_type=MESH,
        ).start()


def halo_arrived(lands, send_sems, recv_sem, me):
    pltpu.make_async_remote_copy(
        src_ref=lands, dst_ref=lands, send_sem=send_sems.at[0], recv_sem=recv_sem,
        device_id=me, device_id_type=MESH,
    ).wait_recv()


def halo_sent(sends, send_sems, me):
    for number, (source, size) in enumerate(((0, Y), (Y, X), (Y + X, X), (0, 1), (Y - 1, 1))):
        part = sends.at[pl.ds(source, size)]
        pltpu.make_async_remote_copy(
            src_ref=part, dst_ref=part, send_sem=send_sems.at[number], recv_sem=send_sems.at[number],
            device_id=me, device_id_type=MESH,
        ).wait_send()


def insert_halo(ext, lands, gx, gy, count):
    front = gx == 1
    back = gx == 0
    below = gy > 0
    above = gy < count - 1

    def put(x, y, cell, valid):
        value = lands[cell].astype(F32)
        ext[pl.ds((x * YE + y) * Q, Q), :] = jnp.where(valid, value, jnp.zeros_like(value))

    for y in range(Y):
        put(0, 1 + y, y, front)
        put(XE - 1, 1 + y, y, back)
    for x in range(X):
        put(1 + x, 0, Y + x, below)
        put(1 + x, YE - 1, Y + X + x, above)
    put(0, 0, 2 * X + Y, front & below)
    put(XE - 1, 0, 2 * X + Y, back & below)
    put(0, YE - 1, 2 * X + Y + 1, front & above)
    put(XE - 1, YE - 1, 2 * X + Y + 1, back & above)


def spread(ext, wide):
    low = low_lanes(Y)
    zero = jnp.zeros((Y, 128), F32)

    @pl.loop(0, XE)
    def _(x):
        rows = pl.ds(pl.multiple_of(x * Y, Y), Y)
        for dy in range(3):
            base = (x * YE + dy) * Q
            pairs = [zero] + [ext[pl.ds(base + q, Y, stride=Q), :] for q in range(Q)] + [zero]
            for q in range(Q):
                mixed = jnp.where(low, pairs[q + 2], pairs[q])
                wide[q, rows, dy * 256 : dy * 256 + 128] = pairs[q + 1].astype(BF16)
                wide[q, rows, dy * 256 + 128 : dy * 256 + 256] = mixed.astype(BF16)


TAPS = ((1, 0), (2, 1), (None, 2), (0, None))


def piece(weight, tap):
    return jnp.zeros((C, C), BF16) if tap is None else weight[tap]


def forward_weight(weight, banded):
    for dy in range(3):
        for slot in range(4):
            rows = slice(dy * 256 + slot * C, dy * 256 + slot * C + C)
            for dx in range(3):
                pieces = [
                    piece(weight, None if t is None else (dx * 3 + dy) * 3 + t) for t in TAPS[slot]
                ]
                banded[rows, dx * 128 : dx * 128 + 128] = jnp.concatenate(pieces, axis=1)


def backward_weight(weight, banded):
    for dx in range(3):
        for b in range(2):
            rows = slice(dx * 128 + b * C, dx * 128 + b * C + C)
            for dy in range(3):
                for half in range(2):
                    pieces = []
                    for slot in (2 * half, 2 * half + 1):
                        t = TAPS[slot][b]
                        tap = None if t is None else ((2 - dx) * 3 + 2 - dy) * 3 + 2 - t
                        pieces.append(piece(weight, tap))
                    start = dy * 256 + half * 128
                    banded[rows, start : start + 128] = jnp.concatenate(pieces, axis=1)


def conv_pair(wide, banded, p, flipped):
    dims = (((1,), (1 if flipped else 0,)), ((), ()))
    result = lax.dot_general(wide[p], banded[...], dims, preferred_element_type=F32)
    n = X * Y
    return result[0:n, 0:128] + result[Y : Y + n, 128:256] + result[2 * Y : 2 * Y + n, 256:384]


def kernel_grad(wide, turned, packed, g):
    low = low_lanes(192)
    turned_value = turned[...]

    def moving(tap):
        dx, dy = tap // 3, tap % 3
        block = wide[:, dx * Y : dx * Y + X * Y, dy * 256 : dy * 256 + 128]
        return block.reshape(Q * X * Y, 128)

    for pair in range(PAIRS):
        first = 2 * pair
        if first + 1 < 9:
            rhs = jnp.concatenate([moving(first), moving(first + 1)], axis=1)
        else:
            rhs = moving(first)
        result = jnp.dot(turned_value, rhs, preferred_element_type=F32)
        one = result[:, 0:128]
        two = result[:, 128:256] if first + 1 < 9 else jnp.zeros_like(one)
        straight = jnp.where(low, one[0:192], two[64:256])
        crossed = jnp.where(low, two[0:192], one[64:256])
        total = straight + pltpu.roll(crossed, 64, 1)
        packed[g, pair * 192 : pair * 192 + 192, :] = total.astype(BF16)


def turn(turned, q, block):
    flat = block.astype(F32).T.astype(BF16)
    columns = lambda w: slice(w * 128, w * 128 + 128)
    turned[64:192, columns(q)] = flat
    if q + 1 < Q:
        turned[0:64, columns(q + 1)] = flat[64:128]
    else:
        turned[192:256, columns(q)] = jnp.zeros((64, 128), BF16)
    if q > 0:
        turned[192:256, columns(q - 1)] = flat[0:64]
    else:
        turned[0:64, columns(q)] = jnp.zeros((64, 128), BF16)


def step(
    sizes, factor,
    field, first, second, cotangent,
    output, first_out, second_out,
    ext_f, ext_c, ext_h, wide_f, wide_c, wide_h,
    banded_1, banded_2, banded_t, turned_c, turned_p, pre,
    sends, lands, packed, mate, part, gathered_xy, summed, gathered_z, final, spread_z, full,
    halo_send, halo_recv, mate_send, mate_recv, xy_send, xy_recv, z_send, z_recv,
    back_z_send, back_z_recv, back_xy_send, back_xy_recv, share_send, share_recv,
):
    nx, ny, ng = sizes
    zl = ng // 2
    nz = nx * zl
    chunk = packed.shape[1] // ny
    tile = chunk // nz
    gx, gy, grp = lax.axis_index("gx"), lax.axis_index("gy"), lax.axis_index("grp")
    core = lax.rem(grp, 2)
    z = gx * zl + grp // 2
    me = (gx, gy, grp)
    sibling = (gx, gy, grp + 1 - 2 * core)

    def along_xy(k):
        return lax.rem(gy + k, ny)

    def along_z(k):
        return lax.rem(z + k, nz)

    def z_device(target):
        return (target // zl, gy, 2 * lax.rem(target, zl) + core)

    barrier = pltpu.get_barrier_semaphore()

    def greet(device):
        pl.semaphore_signal(barrier, inc=1, device_id=device, device_id_type=MESH)

    greet((1 - gx, along_xy(1), grp))
    greet((1 - gx, along_xy(ny - 1), grp))
    greet(sibling)

    @pl.loop(1, nz)
    def _(k):
        greet(z_device(along_z(k)))

    @pl.loop(1, ny)
    def _(k):
        greet((gx, along_xy(k), grp))

    fields = ((field, ext_f, 0), (cotangent, ext_c, 1))
    for source, ext, number in fields:
        for x in range(X):
            for q in range(Q):
                fill_own(ext, x, q, source[0, x, :, q * 128 : q * 128 + 128].astype(F32))
        edge_cells(ext, sends.at[number], gx)
    pl.semaphore_wait(barrier, nz - 1 + ny - 1 + 3)
    for number in range(2):
        halo_copies(
            sends.at[number], lands.at[number], halo_send.at[number], halo_recv.at[number], gx, gy, grp, ny
        )

    forward_weight(first, banded_1)
    forward_weight(second, banded_2)
    backward_weight(second, banded_t)
    for q in range(Q):
        turn(turned_c, q, cotangent[0, :, :, q * 128 : q * 128 + 128].reshape(X * Y, 128))

    halo_arrived(lands.at[0], halo_send.at[0], halo_recv.at[0], me)
    insert_halo(ext_f, lands.at[0], gx, gy, ny)
    spread(ext_f, wide_f)

    @pl.loop(0, Q)
    def _(p):
        value = conv_pair(wide_f, banded_1, p, False)
        pre[p] = value
        hidden = (value * jax.nn.sigmoid(value)).astype(BF16).astype(F32)
        for x in range(X):
            fill_own(ext_h, x, p, hidden[x * Y : x * Y + Y])

    edge_cells(ext_h, sends.at[2], gx)
    halo_copies(sends.at[2], lands.at[2], halo_send.at[2], halo_recv.at[2], gx, gy, grp, ny)

    halo_arrived(lands.at[1], halo_send.at[1], halo_recv.at[1], me)
    insert_halo(ext_c, lands.at[1], gx, gy, ny)
    spread(ext_c, wide_c)
    for p in range(Q):
        hidden_grad = conv_pair(wide_c, banded_t, p, True)
        value = pre[p]
        sigma = jax.nn.sigmoid(value)
        turn(turned_p, p, (hidden_grad * sigma * (1.0 + value * (1.0 - sigma))).astype(BF16))
    if packed.shape[1] > PACKED:
        rest = packed.shape[1] - PACKED
        for g in range(2):
            packed[g, PACKED:, :] = jnp.zeros((rest, 128), BF16)
    kernel_grad(wide_f, turned_p, packed, 0)

    halo_arrived(lands.at[2], halo_send.at[2], halo_recv.at[2], me)
    insert_halo(ext_h, lands.at[2], gx, gy, ny)
    spread(ext_h, wide_h)
    kernel_grad(wide_h, turned_c, packed, 1)

    pair_copy = pltpu.make_async_remote_copy(
        src_ref=packed.at[1 - core], dst_ref=mate, send_sem=mate_send, recv_sem=mate_recv,
        device_id=sibling, device_id_type=MESH,
    )
    pair_copy.start()
    pair_copy.wait_recv()
    part[...] = (packed[core].astype(F32) + mate[...].astype(F32)).astype(BF16)

    @pl.loop(1, ny)
    def _(k):
        to = along_xy(k)
        pltpu.make_async_remote_copy(
            src_ref=part.at[pl.ds(pl.multiple_of(to * chunk, 16), chunk)],
            dst_ref=gathered_xy.at[ny - 1 - k],
            send_sem=xy_send, recv_sem=xy_recv,
            device_id=(gx, to, grp), device_id_type=MESH,
        ).start()

    @pl.loop(0, Q)
    def _(p):
        value = conv_pair(wide_h, banded_2, p, False).astype(BF16)
        columns = pl.ds(pl.multiple_of(p * 128, 128), 128)
        output[0, :, :, columns] = value.reshape(X, Y, 128)

    xy_all = pltpu.make_async_remote_copy(
        src_ref=gathered_xy, dst_ref=gathered_xy, send_sem=xy_send, recv_sem=xy_recv,
        device_id=me, device_id_type=MESH,
    )
    xy_all.wait_recv()
    total = part[pl.ds(pl.multiple_of(gy * chunk, 16), chunk), :].astype(F32)
    for k in range(ny - 1):
        total = total + gathered_xy[k].astype(F32)
    summed[...] = total

    @pl.loop(1, nz)
    def _(k):
        to = along_z(k)
        pltpu.make_async_remote_copy(
            src_ref=summed.at[pl.ds(pl.multiple_of(to * tile, 8), tile)],
            dst_ref=gathered_z.at[nz - 1 - k],
            send_sem=z_send, recv_sem=z_recv,
            device_id=z_device(to), device_id_type=MESH,
        ).start()

    z_all = pltpu.make_async_remote_copy(
        src_ref=gathered_z, dst_ref=gathered_z, send_sem=z_send, recv_sem=z_recv,
        device_id=me, device_id_type=MESH,
    )
    z_all.wait_recv()
    own_rows = pl.ds(pl.multiple_of(z * tile, 8), tile)
    mine = summed[own_rows, :]
    for k in range(nz - 1):
        mine = mine + gathered_z[k]
    final[...] = mine
    spread_z[own_rows, :] = mine

    @pl.loop(1, nz)
    def _(k):
        pltpu.make_async_remote_copy(
            src_ref=final, dst_ref=spread_z.at[own_rows],
            send_sem=back_z_send, recv_sem=back_z_recv,
            device_id=z_device(along_z(k)), device_id_type=MESH,
        ).start()

    pltpu.make_async_remote_copy(
        src_ref=gathered_z, dst_ref=gathered_z, send_sem=back_z_send, recv_sem=back_z_recv,
        device_id=me, device_id_type=MESH,
    ).wait_recv()

    def rows_of(j):
        return pl.ds(pl.multiple_of(j * chunk, 16), chunk)

    full[core, rows_of(gy), :] = spread_z[...].astype(BF16)

    @pl.loop(1, ny)
    def _(k):
        pltpu.make_async_remote_copy(
            src_ref=full.at[core, rows_of(gy)], dst_ref=full.at[core, rows_of(gy)],
            send_sem=back_xy_send, recv_sem=back_xy_recv.at[k],
            device_id=(gx, along_xy(k), grp), device_id_type=MESH,
        ).start()

    def share(j):
        pltpu.make_async_remote_copy(
            src_ref=full.at[core, rows_of(j)], dst_ref=full.at[core, rows_of(j)],
            send_sem=share_send, recv_sem=share_recv,
            device_id=sibling, device_id_type=MESH,
        ).start()

    share(gy)

    @pl.loop(1, ny)
    def _(k):
        j = along_xy(ny - k)
        pltpu.make_async_remote_copy(
            src_ref=full.at[core, rows_of(j)], dst_ref=full.at[core, rows_of(j)],
            send_sem=back_xy_send, recv_sem=back_xy_recv.at[k],
            device_id=me, device_id_type=MESH,
        ).wait_recv()
        share(j)

    whole = pltpu.make_async_remote_copy(
        src_ref=full.at[core], dst_ref=full.at[1 - core], send_sem=share_send, recv_sem=share_recv,
        device_id=sibling, device_id_type=MESH,
    )
    whole.wait_recv()

    rows = lax.broadcasted_iota(jnp.int32, (128, 128), 0)
    lanes = lax.broadcasted_iota(jnp.int32, (128, 128), 1)
    unit = (rows == lanes).astype(BF16)
    for g, target in ((0, first_out), (1, second_out)):
        for pair in range(PAIRS):
            for v in range(3):
                start = pair * 192 + v * 64
                block = lax.dot_general(
                    unit, full[g, start : start + 64, :], (((1,), (1,)), ((), ())),
                    preferred_element_type=F32,
                ) * factor
                for half in range(2):
                    tap = 2 * pair + half
                    if tap < 9:
                        target[tap * 3 + 2 - v] = block[half * 64 : half * 64 + 64]

    for number in range(3):
        halo_sent(sends.at[number], halo_send.at[number], me)
    pair_copy.wait_send()
    xy_all.wait_send()
    z_all.wait_send()
    pltpu.make_async_remote_copy(
        src_ref=gathered_z, dst_ref=gathered_z, send_sem=back_z_send, recv_sem=back_z_recv,
        device_id=me, device_id_type=MESH,
    ).wait_send()
    pltpu.make_async_remote_copy(
        src_ref=gathered_xy, dst_ref=gathered_xy, send_sem=back_xy_send, recv_sem=xy_recv,
        device_id=me, device_id_type=MESH,
    ).wait_send()
    whole.wait_send()


def shards(sizes, field_in, first_weight, second_weight, cotangent):
    nx, ny, ng = sizes
    nz = nx * ng // 2
    tile = 8 * pl.cdiv(pl.cdiv(PACKED, 8), ny * nz)
    chunk = tile * nz
    rows = chunk * ny
    total = ng * nx * X * ny * Y * NZ
    dma = pltpu.SemaphoreType.DMA
    vmem = pltpu.VMEM
    whole = pl.BlockSpec(memory_space=pltpu.VMEM)
    cells = (XE * YE * Q, 128)
    wide = (Q, ROWS_E, 768)
    output, first_grad, second_grad = pl.pallas_call(
        functools.partial(step, sizes, 1.0 / math.sqrt(total)),
        out_shape=(
            jax.ShapeDtypeStruct(field_in.shape, BF16),
            jax.ShapeDtypeStruct((27, C, C), F32),
            jax.ShapeDtypeStruct((27, C, C), F32),
        ),
        in_specs=[whole] * 4,
        out_specs=(whole,) * 3,
        scratch_shapes=[
            vmem(cells, F32), vmem(cells, F32), vmem(cells, F32),
            vmem(wide, BF16), vmem(wide, BF16), vmem(wide, BF16),
            vmem((768, 384), BF16), vmem((768, 384), BF16), vmem((384, 768), BF16),
            vmem((256, Q * 128), BF16), vmem((256, Q * 128), BF16),
            vmem((Q, X * Y, 128), F32),
            vmem((3, 2 * X + Y, Q, 128), BF16), vmem((3, CELLS, Q, 128), BF16),
            vmem((2, rows, 128), BF16), vmem((rows, 128), BF16), vmem((rows, 128), BF16),
            vmem((ny - 1, chunk, 128), BF16), vmem((chunk, 128), F32),
            vmem((nz - 1, tile, 128), F32), vmem((tile, 128), F32), vmem((chunk, 128), F32),
            vmem((2, rows, 128), BF16),
            dma((3, 5)), dma((3,)), dma, dma, dma, dma, dma, dma,
            dma, dma, dma, dma((ny,)), dma, dma,
        ],
        compiler_params=pltpu.CompilerParams(
            collective_id=0, has_side_effects=True, vmem_limit_bytes=48 * 1024 * 1024
        ),
    )(
        field_in,
        first_weight.reshape(27, C, C),
        second_weight.reshape(27, C, C),
        cotangent,
    )
    shape = (3, 3, 3, C, C)
    return output, first_grad.reshape(shape), second_grad.reshape(shape)


def solution(mesh):
    sizes = (mesh.shape["gx"], mesh.shape["gy"], mesh.shape["grp"])
    return jax.shard_map(
        functools.partial(shards, sizes),
        mesh=mesh,
        in_specs=(P("grp", "gx", "gy", None), P(), P(), P("grp", "gx", "gy", None)),
        out_specs=(P("grp", "gx", "gy", None), P(), P()),
        check_vma=False,
    )
```

time: 422 us -> 62.4 us (0.15)
  waiting for transfers between devices: 264 us -> 0 us
  Pallas kernels: 0 us -> 55 us
  matrix products: 49.5 us -> 0 us
  starting transfers between devices: 46.6 us -> 0 us
  local copies, waits for them, and re-layouts: 39.2 us -> 6.45 us
  between operations: 15 us -> 0.65 us
  other arithmetic: 4.27 us -> 0 us
    psum x1 -> x0, waiting for transfers between devices: 264 us -> none  [reduce_grad(): return lax.psum(local, ('gx', 'gy', 'grp'))]
    pallas_call x0 -> x1, Pallas kernels: none -> 55 us  [shards(): pl.pallas_call(functools.partial(step, sizes, 1.0 / math.sqrt(total)), ou...]
    ppermute x12 -> x0, starting transfers between devices: 46.6 us -> none  [the longest x6 38.6 us: extended(): lax.ppermute(tail, axis, [(i, (i + 1) % count) for i in range(ends)])]
    transpose x2 -> x0, matrix products: 41.1 us -> none  [kernel_local(): return jnp.transpose(result, (1, 2, 3, 0, 4))]
    reshape x15 -> x0, local copies, waits for them, and re-layouts: 18.9 us -> none  [the longest x13 16.8 us: as_cells(): return field.reshape(field.shape[0], field.shape[1], field.shape[2], NZ, C)]
    conv_general_dilated x2 -> x0, matrix products: 8.46 us -> none  [conv_local(): lax.conv_general_dilated(padded, weight, (1, 1, 1), ((0, 0), (0, 0), (1,...]
    conv_general_dilated x9 -> x0, local copies, waits for them, and re-layouts: 6.24 us -> none  [conv_local(): lax.conv_general_dilated(padded, weight, (1, 1, 1), ((0, 0), (0, 0), (1,...]
    unnamed x50 -> x11, local copies, waits for them, and re-layouts: 9.51 us -> 6.45 us
  transfers between devices with their start and end apart: 13 -> 0, of which waited for: 1 -> 0; matrix products, arithmetic and copies ran while one was open for 15% -> 0% of each run, Pallas kernels for 0% -> 0%
where the time goes in v1:
time: 62.4 us; the launch traced here: 62.1 us
  Pallas kernels  55 us (88%)
  local copies, waits for them, and re-layouts  6.45 us (10%)
  between operations  0.65 us (1%)
    pallas_call x1, Pallas kernels, shards(): pl.pallas_call(functools.partial(step, sizes, 1.0 / math.sqrt(total)), ou...  55 us
    unnamed x11, local copies, waits for them, and re-layouts  6.45 us

profile of v1, /device:TPU:1, one launch (start us, length us, event | category | flops | bytes accessed | tf_op | source)
XLA Modules:
  0.0 62.1 jit_solution(2779743026817352414)
XLA Ops:
  0.6 0.0 copy-start
  0.6 1.0 %copy-done = bf16[3,3,3,64,64]{4,3,2,1,0:T(8,128)(2,1)S(1)} copy-done((bf16[3,3,3,64,64]{4,3,2,1,0:T(8,128)(2,1)S(1)}, bf16[3,3,3,64,64]{4,3,2,1,0:T(8,128)(2,1)}, u32[]{:S(2)}) %copy-start) | copy-done | bytes 221208
  1.6 0.0 copy-start.1
  1.6 1.0 %copy-done.1 = bf16[3,3,3,64,64]{4,3,2,1,0:T(8,128)(2,1)S(1)} copy-done((bf16[3,3,3,64,64]{4,3,2,1,0:T(8,128)(2,1)S(1)}, bf16[3,3,3,64,64]{4,3,2,1,0:T(8,128)(2,1)}, u32[]{:S(2)}) %copy-start.1) | copy-done | bytes 221208
  2.7 0.0 copy-start.2
  2.7 0.9 %copy-done.2 = bf16[1,8,16,1024]{3,2,1,0:T(8,128)(2,1)S(1)} copy-done((bf16[1,8,16,1024]{3,2,1,0:T(8,128)(2,1)S(1)}, bf16[1,8,16,1024]{3,2,1,0:T(8,128)(2,1)}, u32[]{:S(2)}) %copy-start.2) | copy-done | bytes 262168
  3.6 0.0 copy-start.3
  3.6 0.9 %copy-done.3 = bf16[1,8,16,1024]{3,2,1,0:T(8,128)(2,1)S(1)} copy-done((bf16[1,8,16,1024]{3,2,1,0:T(8,128)(2,1)S(1)}, bf16[1,8,16,1024]{3,2,1,0:T(8,128)(2,1)}, u32[]{:S(2)}) %copy-start.3) | copy-done | bytes 262168
  4.6 55.0 %shard_map.67 = (bf16[1,8,16,1024]{3,2,1,0:T(8,128)(2,1)S(1)}, f32[27,64,64]{2,1,0:T(8,128)S(1)}, f32[27,64,64]{2,1,0:T(8,128)S(1)}) custom-call(bf16[1,8,16,1024]{3,2,1,0:T(8,128)(2,1)S(1)} %copy-done.2, bf16[27,64,64]{2,1,0:T(8,128)(2,1)S(1)} %bitcast.6, bf16[27,64,64]{2,1,0:T(8,128)(2,1)S(1)} %bitcast.7, bf16[1,8,16,1024]{3,2,1,0:T(8,128)(2,1)S(1)} %copy-done.3), custom_call_target="tpu_custom_call" | custom-call | tf_op jit(solution)/shard_map/pallas_call | solution.py:449
  59.6 0.7 %copy.10 = bf16[1,8,16,1024]{3,2,1,0:T(8,128)(2,1)} copy(bf16[1,8,16,1024]{3,2,1,0:T(8,128)(2,1)S(1)} %get-tuple-element.12) | data formatting | bytes 524288
  60.3 0.9 %copy.11 = f32[3,3,3,64,64]{4,3,2,1,0:T(8,128)} copy(f32[3,3,3,64,64]{4,3,2,1,0:T(8,128)S(1)} %bitcast.5) | data formatting | bytes 884736
  61.2 0.9 %copy.12 = f32[3,3,3,64,64]{4,3,2,1,0:T(8,128)} copy(f32[3,3,3,64,64]{4,3,2,1,0:T(8,128)S(1)} %bitcast.4) | data formatting | bytes 884736
Async XLA Ops:
  0.6 1.0 %copy-start = (bf16[3,3,3,64,64]{4,3,2,1,0:T(8,128)(2,1)S(1)}, bf16[3,3,3,64,64]{4,3,2,1,0:T(8,128)(2,1)}, u32[]{:S(2)}) copy-start(bf16[3,3,3,64,64]{4,3,2,1,0:T(8,128)(2,1)} %param.5) | copy-start | bytes 663556
  1.6 1.0 %copy-start.1 = (bf16[3,3,3,64,64]{4,3,2,1,0:T(8,128)(2,1)S(1)}, bf16[3,3,3,64,64]{4,3,2,1,0:T(8,128)(2,1)}, u32[]{:S(2)}) copy-start(bf16[3,3,3,64,64]{4,3,2,1,0:T(8,128)(2,1)} %param.6) | copy-start | bytes 663556
  2.7 0.9 %copy-start.2 = (bf16[1,8,16,1024]{3,2,1,0:T(8,128)(2,1)S(1)}, bf16[1,8,16,1024]{3,2,1,0:T(8,128)(2,1)}, u32[]{:S(2)}) copy-start(bf16[1,8,16,1024]{3,2,1,0:T(8,128)(2,1)} %field.1) | copy-start | bytes 786436
  3.6 0.9 %copy-start.3 = (bf16[1,8,16,1024]{3,2,1,0:T(8,128)(2,1)S(1)}, bf16[1,8,16,1024]{3,2,1,0:T(8,128)(2,1)}, u32[]{:S(2)}) copy-start(bf16[1,8,16,1024]{3,2,1,0:T(8,128)(2,1)} %cotangent.1) | copy-start | bytes 786436

commit v2 on v1

--- a/solution.py
+++ b/solution.py
@@ -151,11 +151,20 @@
                     banded[rows, start : start + 128] = jnp.concatenate(pieces, axis=1)
 
 
-def conv_pair(wide, banded, p, flipped):
+def conv_all(wide, banded, shifted, flipped):
     dims = (((1,), (1 if flipped else 0,)), ((), ()))
-    result = lax.dot_general(wide[p], banded[...], dims, preferred_element_type=F32)
+    rows = wide[...].reshape(Q * ROWS_E, 768)
+    result = lax.dot_general(rows, banded[...], dims, preferred_element_type=F32)
+    shifted[...] = result.reshape(Q, ROWS_E, 384)
+
+
+def conv_pair(shifted, p):
     n = X * Y
-    return result[0:n, 0:128] + result[Y : Y + n, 128:256] + result[2 * Y : 2 * Y + n, 256:384]
+    return (
+        shifted[p, 0:n, 0:128]
+        + shifted[p, Y : Y + n, 128:256]
+        + shifted[p, 2 * Y : 2 * Y + n, 256:384]
+    )
 
 
 def kernel_grad(wide, turned, packed, g):
@@ -197,20 +206,28 @@
 
 
 def step(
-    sizes, factor,
-    field, first, second, cotangent,
-    output, first_out, second_out,
+    sizes,
+    field_hbm, first_hbm, second_hbm, cotangent_hbm,
+    output, full,
+    field, first, second, cotangent, load_sems, shifted,
     ext_f, ext_c, ext_h, wide_f, wide_c, wide_h,
     banded_1, banded_2, banded_t, turned_c, turned_p, pre,
-    sends, lands, packed, mate, part, gathered_xy, summed, gathered_z, final, spread_z, full,
+    sends, lands, packed, mate, part, gathered_xy, gathered_z,
     halo_send, halo_recv, mate_send, mate_recv, xy_send, xy_recv, z_send, z_recv,
-    back_z_send, back_z_recv, back_xy_send, back_xy_recv, share_send, share_recv,
+    back_xy_send, back_xy_recv, share_send, share_recv,
 ):
     nx, ny, ng = sizes
     zl = ng // 2
     nz = nx * zl
     chunk = packed.shape[1] // ny
-    tile = chunk // nz
+    loads = [
+        pltpu.make_async_copy(source, target, load_sems.at[number])
+        for number, (source, target) in enumerate(
+            ((field_hbm, field), (cotangent_hbm, cotangent), (first_hbm, first), (second_hbm, second))
+        )
+    ]
+    for load in loads:
+        load.start()
     gx, gy, grp = lax.axis_index("gx"), lax.axis_index("gy"), lax.axis_index("grp")
     core = lax.rem(grp, 2)
     z = gx * zl + grp // 2
@@ -245,6 +262,7 @@
 
     fields = ((field, ext_f, 0), (cotangent, ext_c, 1))
     for source, ext, number in fields:
+        loads[number].wait()
         for x in range(X):
             for q in range(Q):
                 fill_own(ext, x, q, source[0, x, :, q * 128 : q * 128 + 128].astype(F32))
@@ -255,6 +273,8 @@
             sends.at[number], lands.at[number], halo_send.at[number], halo_recv.at[number], gx, gy, grp, ny
         )
 
+    loads[2].wait()
+    loads[3].wait()
     forward_weight(first, banded_1)
     forward_weight(second, banded_2)
     backward_weight(second, banded_t)
@@ -265,9 +285,11 @@
     insert_halo(ext_f, lands.at[0], gx, gy, ny)
     spread(ext_f, wide_f)
 
+    conv_all(wide_f, banded_1, shifted, False)
+
     @pl.loop(0, Q)
     def _(p):
-        value = conv_pair(wide_f, banded_1, p, False)
+        value = conv_pair(shifted, p)
         pre[p] = value
         hidden = (value * jax.nn.sigmoid(value)).astype(BF16).astype(F32)
         for x in range(X):
@@ -279,8 +301,9 @@
     halo_arrived(lands.at[1], halo_send.at[1], halo_recv.at[1], me)
     insert_halo(ext_c, lands.at[1], gx, gy, ny)
     spread(ext_c, wide_c)
+    conv_all(wide_c, banded_t, shifted, True)
     for p in range(Q):
-        hidden_grad = conv_pair(wide_c, banded_t, p, True)
+        hidden_grad = conv_pair(shifted, p)
         value = pre[p]
         sigma = jax.nn.sigmoid(value)
         turn(turned_p, p, (hidden_grad * sigma * (1.0 + value * (1.0 - sigma))).astype(BF16))
@@ -313,9 +336,11 @@
             device_id=(gx, to, grp), device_id_type=MESH,
         ).start()
 
+    conv_all(wide_h, banded_2, shifted, False)
+
     @pl.loop(0, Q)
     def _(p):
-        value = conv_pair(wide_h, banded_2, p, False).astype(BF16)
+        value = conv_pair(shifted, p).astype(BF16)
         columns = pl.ds(pl.multiple_of(p * 128, 128), 128)
         output[0, :, :, columns] = value.reshape(X, Y, 128)
 
@@ -327,47 +352,30 @@
     total = part[pl.ds(pl.multiple_of(gy * chunk, 16), chunk), :].astype(F32)
     for k in range(ny - 1):
         total = total + gathered_xy[k].astype(F32)
-    summed[...] = total
+    gathered_z[z] = total.astype(BF16)
 
     @pl.loop(1, nz)
     def _(k):
-        to = along_z(k)
-        pltpu.make_async_remote_copy(
-            src_ref=summed.at[pl.ds(pl.multiple_of(to * tile, 8), tile)],
-            dst_ref=gathered_z.at[nz - 1 - k],
+        pltpu.make_async_remote_copy(
+            src_ref=gathered_z.at[z], dst_ref=gathered_z.at[z],
             send_sem=z_send, recv_sem=z_recv,
-            device_id=z_device(to), device_id_type=MESH,
-        ).start()
-
-    z_all = pltpu.make_async_remote_copy(
-        src_ref=gathered_z, dst_ref=gathered_z, send_sem=z_send, recv_sem=z_recv,
-        device_id=me, device_id_type=MESH,
-    )
-    z_all.wait_recv()
-    own_rows = pl.ds(pl.multiple_of(z * tile, 8), tile)
-    mine = summed[own_rows, :]
-    for k in range(nz - 1):
-        mine = mine + gathered_z[k]
-    final[...] = mine
-    spread_z[own_rows, :] = mine
-
-    @pl.loop(1, nz)
-    def _(k):
-        pltpu.make_async_remote_copy(
-            src_ref=final, dst_ref=spread_z.at[own_rows],
-            send_sem=back_z_send, recv_sem=back_z_recv,
             device_id=z_device(along_z(k)), device_id_type=MESH,
         ).start()
 
-    pltpu.make_async_remote_copy(
-        src_ref=gathered_z, dst_ref=gathered_z, send_sem=back_z_send, recv_sem=back_z_recv,
+    others = gathered_z.at[pl.ds(0, nz - 1)]
+    z_all = pltpu.make_async_remote_copy(
+        src_ref=others, dst_ref=others, send_sem=z_send, recv_sem=z_recv,
         device_id=me, device_id_type=MESH,
-    ).wait_recv()
+    )
+    z_all.wait_recv()
+    grand = gathered_z[0].astype(F32)
+    for k in range(1, nz):
+        grand = grand + gathered_z[k].astype(F32)
 
     def rows_of(j):
         return pl.ds(pl.multiple_of(j * chunk, 16), chunk)
 
-    full[core, rows_of(gy), :] = spread_z[...].astype(BF16)
+    full[core, rows_of(gy), :] = grand.astype(BF16)
 
     @pl.loop(1, ny)
     def _(k):
@@ -402,10 +410,30 @@
     )
     whole.wait_recv()
 
+    for number in range(3):
+        halo_sent(sends.at[number], halo_send.at[number], me)
+    pair_copy.wait_send()
+    xy_all.wait_send()
+    z_all.wait_send()
+    pltpu.make_async_remote_copy(
+        src_ref=gathered_xy, dst_ref=gathered_xy, send_sem=back_xy_send, recv_sem=xy_recv,
+        device_id=me, device_id_type=MESH,
+    ).wait_send()
+    whole.wait_send()
+
+
+def unpack(factor, output_in, full, output, first_out, second_out, one, two, sems):
+    copies = [
+        pltpu.make_async_copy(source, target, sems.at[number])
+        for number, (source, target) in enumerate(
+            ((output_in, output), (one, first_out), (two, second_out))
+        )
+    ]
+    copies[0].start()
     rows = lax.broadcasted_iota(jnp.int32, (128, 128), 0)
     lanes = lax.broadcasted_iota(jnp.int32, (128, 128), 1)
     unit = (rows == lanes).astype(BF16)
-    for g, target in ((0, first_out), (1, second_out)):
+    for g, target in ((0, one), (1, two)):
         for pair in range(PAIRS):
             for v in range(3):
                 start = pair * 192 + v * 64
@@ -417,45 +445,35 @@
                     tap = 2 * pair + half
                     if tap < 9:
                         target[tap * 3 + 2 - v] = block[half * 64 : half * 64 + 64]
-
-    for number in range(3):
-        halo_sent(sends.at[number], halo_send.at[number], me)
-    pair_copy.wait_send()
-    xy_all.wait_send()
-    z_all.wait_send()
-    pltpu.make_async_remote_copy(
-        src_ref=gathered_z, dst_ref=gathered_z, send_sem=back_z_send, recv_sem=back_z_recv,
-        device_id=me, device_id_type=MESH,
-    ).wait_send()
-    pltpu.make_async_remote_copy(
-        src_ref=gathered_xy, dst_ref=gathered_xy, send_sem=back_xy_send, recv_sem=xy_recv,
-        device_id=me, device_id_type=MESH,
-    ).wait_send()
-    whole.wait_send()
+        copies[g + 1].start()
+    for copy in copies:
+        copy.wait()
 
 
 def shards(sizes, field_in, first_weight, second_weight, cotangent):
     nx, ny, ng = sizes
     nz = nx * ng // 2
-    tile = 8 * pl.cdiv(pl.cdiv(PACKED, 8), ny * nz)
-    chunk = tile * nz
+    chunk = 16 * pl.cdiv(PACKED, 16 * ny)
     rows = chunk * ny
     total = ng * nx * X * ny * Y * NZ
     dma = pltpu.SemaphoreType.DMA
     vmem = pltpu.VMEM
-    whole = pl.BlockSpec(memory_space=pltpu.VMEM)
+    inside = pl.BlockSpec(memory_space=pltpu.VMEM)
+    outside = pl.BlockSpec(memory_space=pltpu.HBM)
     cells = (XE * YE * Q, 128)
     wide = (Q, ROWS_E, 768)
-    output, first_grad, second_grad = pl.pallas_call(
-        functools.partial(step, sizes, 1.0 / math.sqrt(total)),
+    weight = (27, C, C)
+    output, full = pl.pallas_call(
+        functools.partial(step, sizes),
         out_shape=(
             jax.ShapeDtypeStruct(field_in.shape, BF16),
-            jax.ShapeDtypeStruct((27, C, C), F32),
-            jax.ShapeDtypeStruct((27, C, C), F32),
+            jax.ShapeDtypeStruct((2, rows, 128), BF16),
         ),
-        in_specs=[whole] * 4,
-        out_specs=(whole,) * 3,
+        in_specs=[outside] * 4,
+        out_specs=(inside,) * 2,
         scratch_shapes=[
+            vmem(field_in.shape, BF16), vmem(weight, BF16), vmem(weight, BF16), vmem(field_in.shape, BF16),
+            dma((4,)), vmem((Q, ROWS_E, 384), F32),
             vmem(cells, F32), vmem(cells, F32), vmem(cells, F32),
             vmem(wide, BF16), vmem(wide, BF16), vmem(wide, BF16),
             vmem((768, 384), BF16), vmem((768, 384), BF16), vmem((384, 768), BF16),
@@ -463,21 +481,36 @@
             vmem((Q, X * Y, 128), F32),
             vmem((3, 2 * X + Y, Q, 128), BF16), vmem((3, CELLS, Q, 128), BF16),
             vmem((2, rows, 128), BF16), vmem((rows, 128), BF16), vmem((rows, 128), BF16),
-            vmem((ny - 1, chunk, 128), BF16), vmem((chunk, 128), F32),
-            vmem((nz - 1, tile, 128), F32), vmem((tile, 128), F32), vmem((chunk, 128), F32),
-            vmem((2, rows, 128), BF16),
+            vmem((ny - 1, chunk, 128), BF16), vmem((nz, chunk, 128), BF16),
             dma((3, 5)), dma((3,)), dma, dma, dma, dma, dma, dma,
-            dma, dma, dma, dma((ny,)), dma, dma,
+            dma, dma((ny,)), dma, dma,
         ],
         compiler_params=pltpu.CompilerParams(
-            collective_id=0, has_side_effects=True, vmem_limit_bytes=48 * 1024 * 1024
+            collective_id=0, has_side_effects=True, vmem_limit_bytes=40 * 1024 * 1024
         ),
     )(
-        field_in,
-        first_weight.reshape(27, C, C),
-        second_weight.reshape(27, C, C),
-        cotangent,
-    )
+        *(
+            pltpu.with_memory_space_constraint(array, pltpu.HBM)
+            for array in (
+                field_in,
+                first_weight.reshape(weight),
+                second_weight.reshape(weight),
+                cotangent,
+            )
+        )
+    )
+    output, first_grad, second_grad = pl.pallas_call(
+        functools.partial(unpack, 1.0 / math.sqrt(total)),
+        out_shape=(
+            jax.ShapeDtypeStruct(field_in.shape, BF16),
+            jax.ShapeDtypeStruct(weight, F32),
+            jax.ShapeDtypeStruct(weight, F32),
+        ),
+        in_specs=[inside] * 2,
+        out_specs=(outside,) * 3,
+        scratch_shapes=[vmem(weight, F32), vmem(weight, F32), dma((3,))],
+        compiler_params=pltpu.CompilerParams(vmem_limit_bytes=16 * 1024 * 1024),
+    )(output, full)
     shape = (3, 3, 3, C, C)
     return output, first_grad.reshape(shape), second_grad.reshape(shape)
 

time: 62.4 us -> 52.3 us (0.84)
  local copies, waits for them, and re-layouts: 6.45 us -> 0 us
  Pallas kernels: 55 us -> 51.6 us
    unnamed x11 -> x0, local copies, waits for them, and re-layouts: 6.45 us -> none
    pallas_call x1 -> x2, Pallas kernels: 55 us -> 51.6 us  [the longest x1 50 us: shards(): pl.pallas_call(functools.partial(step, sizes), out_shape=(jax.ShapeDtypeS...]
where the time goes in v2:
time: 52.3 us; the launch traced here: 52.2 us
  Pallas kernels  51.6 us (99%)
  between operations  0.64 us (1%)
    pallas_call x1, Pallas kernels, shards(): pl.pallas_call(functools.partial(step, sizes), out_shape=(jax.ShapeDtypeS...  50 us
    pallas_call x1, Pallas kernels, shards(): pl.pallas_call(functools.partial(unpack, 1.0 / math.sqrt(total)), out_sha...  1.51 us

profile of v2, /device:TPU:1, one launch (start us, length us, event | category | flops | bytes accessed | tf_op | source)
XLA Modules:
  0.0 52.2 jit_solution(8600239630354730403)
XLA Ops:
  0.6 50.0 %shard_map.67 = (bf16[1,8,16,1024]{3,2,1,0:T(8,128)(2,1)S(1)}, bf16[2,1024,128]{2,1,0:T(8,128)(2,1)S(1)}) custom-call(bf16[1,8,16,1024]{3,2,1,0:T(8,128)(2,1)} %field_hbm.1, bf16[27,64,64]{2,1,0:T(8,128)(2,1)} %bitcast.4, bf16[27,64,64]{2,1,0:T(8,128)(2,1)} %bitcast.5, bf16[1,8,16,1024]{3,2,1,0:T(8,128)(2,1)} %cotangent_hbm.1), custom_call_target="tpu_custom_call" | custom-call | tf_op jit(solution)/shard_map/pallas_call | solution.py:466
  50.7 1.5 %shard_map.68 = (bf16[1,8,16,1024]{3,2,1,0:T(8,128)(2,1)}, f32[27,64,64]{2,1,0:T(8,128)}, f32[27,64,64]{2,1,0:T(8,128)}) custom-call(bf16[1,8,16,1024]{3,2,1,0:T(8,128)(2,1)S(1)} %get-tuple-element.8.output_in, bf16[2,1024,128]{2,1,0:T(8,128)(2,1)S(1)} %get-tuple-element.9.full), custom_call_target="tpu_custom_call" | custom-call | tf_op jit(solution)/shard_map/pallas_call | solution.py:502

commit v3 on v2

--- a/solution.py
+++ b/solution.py
@@ -14,11 +14,10 @@
 Y = 16
 Q = 8
 XE = X + 2
-YE = Y + 2
+SLOT = 32
 ROWS_E = XE * Y
 PAIRS = 5
 PACKED = PAIRS * 192
-CELLS = 2 * X + Y + 2
 F32 = jnp.float32
 BF16 = jnp.bfloat16
 MESH = pl.DeviceIdType.MESH
@@ -28,94 +27,151 @@
     return lax.broadcasted_iota(jnp.int32, (rows, 128), 1) < 64
 
 
-def fill_own(ext, x, q, value):
-    ext[pl.ds(((x + 1) * YE + 1) * Q + q, Y, stride=Q), :] = value
-
-
-def edge_cells(ext, sends, gx):
+def row(q, x, y):
+    return (q * XE + x) * SLOT + 8 + y
+
+
+def clear_halo(ext, shifted):
+    edge = jnp.zeros((8, 128), F32)
+    plane = jnp.zeros((SLOT, 128), F32)
+    for q in range(Q):
+        for x in range(XE):
+            if x in (0, XE - 1):
+                ext[pl.ds(row(q, x, -8), SLOT), :] = plane
+            else:
+                ext[pl.ds(row(q, x, -8), 8), :] = edge
+                ext[pl.ds(row(q, x, Y), 8), :] = edge
+        shifted[q, 0:Y, :] = jnp.zeros((Y, 384), F32)
+        shifted[q, ROWS_E - Y : ROWS_E, :] = jnp.zeros((Y, 384), F32)
+
+
+def take_edges(ext, send_x, send_y, send_c, corner, gx):
     near = X - (X - 1) * gx
-    for y in range(Y):
-        start = pl.multiple_of((near * YE + 1 + y) * Q, Q)
-        sends[y] = ext[pl.ds(start, Q), :].astype(BF16)
-    for x in range(X):
-        sends[Y + x] = ext[pl.ds(((x + 1) * YE + 1) * Q, Q), :].astype(BF16)
-        sends[Y + X + x] = ext[pl.ds(((x + 1) * YE + Y) * Q, Q), :].astype(BF16)
-
-
-def halo_copies(sends, lands, send_sems, recv_sem, gx, gy, grp, count):
+    for q in range(Q):
+        columns = slice(q * 128, q * 128 + 128)
+        plane = ext[pl.ds(pl.multiple_of(row(q, near, 0), 8), Y), :]
+        send_x[:, columns] = plane.astype(BF16)
+        corner[0, q : q + 1, :] = plane[0:1]
+        corner[1, q : q + 1, :] = plane[Y - 1 : Y]
+        for side, y in ((0, 0), (1, Y - 1)):
+            send_y[side, :, columns] = ext[pl.ds(row(q, 1, y), X, stride=SLOT), :].astype(BF16)
+    send_c[...] = corner[...].astype(BF16)
+
+
+def halo_copies(ends, send_sems, recv_sems, place, count):
+    send_x, send_y, send_c, land_x, land_y, land_c = ends
+    gx, gy, grp = place
     up = lax.rem(gy + 1, count)
     down = lax.rem(gy + count - 1, count)
-    other = 1 - gx
     moves = (
-        (0, Y, 0, other, gy),
-        (Y, X, Y + X, gx, down),
-        (Y + X, X, Y, gx, up),
-        (0, 1, 2 * X + Y + 1, other, down),
-        (Y - 1, 1, 2 * X + Y, other, up),
-    )
-    for number, (source, size, target, to_x, to_y) in enumerate(moves):
+        (send_x, land_x, (1 - gx, gy, grp)),
+        (send_y.at[1], land_y.at[0], (gx, up, grp)),
+        (send_y.at[0], land_y.at[1], (gx, down, grp)),
+        (send_c.at[1], land_c.at[0], (1 - gx, up, grp)),
+        (send_c.at[0], land_c.at[1], (1 - gx, down, grp)),
+    )
+    return [
         pltpu.make_async_remote_copy(
-            src_ref=sends.at[pl.ds(source, size)],
-            dst_ref=lands.at[pl.ds(target, size)],
-            send_sem=send_sems.at[number],
-            recv_sem=recv_sem,
-            device_id=(to_x, to_y, grp),
-            device_id_type=MESH,
-        ).start()
-
-
-def halo_arrived(lands, send_sems, recv_sem, me):
-    pltpu.make_async_remote_copy(
-        src_ref=lands, dst_ref=lands, send_sem=send_sems.at[0], recv_sem=recv_sem,
-        device_id=me, device_id_type=MESH,
-    ).wait_recv()
-
-
-def halo_sent(sends, send_sems, me):
-    for number, (source, size) in enumerate(((0, Y), (Y, X), (Y + X, X), (0, 1), (Y - 1, 1))):
-        part = sends.at[pl.ds(source, size)]
-        pltpu.make_async_remote_copy(
-            src_ref=part, dst_ref=part, send_sem=send_sems.at[number], recv_sem=send_sems.at[number],
-            device_id=me, device_id_type=MESH,
-        ).wait_send()
-
-
-def insert_halo(ext, lands, gx, gy, count):
-    front = gx == 1
-    back = gx == 0
-    below = gy > 0
-    above = gy < count - 1
-
-    def put(x, y, cell, valid):
-        value = lands[cell].astype(F32)
-        ext[pl.ds((x * YE + y) * Q, Q), :] = jnp.where(valid, value, jnp.zeros_like(value))
-
-    for y in range(Y):
-        put(0, 1 + y, y, front)
-        put(XE - 1, 1 + y, y, back)
+            src_ref=source, dst_ref=target, send_sem=send_sems.at[number], recv_sem=recv_sems.at[number],
+            device_id=device, device_id_type=MESH,
+        )
+        for number, (source, target, device) in enumerate(moves)
+    ]
+
+
+def insert_y(ext, land_y, sided):
+    for side, y in ((0, -1), (1, Y)):
+        for q in range(Q):
+            value = land_y[side, :, q * 128 : q * 128 + 128].astype(F32)
+            value = jnp.where(sided[side], value, jnp.zeros_like(value))
+            ext[pl.ds(row(q, 1, y), X, stride=SLOT), :] = value
+
+
+def insert_x(ext, land_x, land_c, sided, far, corner):
+    corner[...] = land_c[...].astype(F32)
+    for q in range(Q):
+        start = pl.multiple_of(row(q, far, 0), 8)
+        ext[pl.ds(start, Y), :] = land_x[:, q * 128 : q * 128 + 128].astype(F32)
+        low = corner[0, q : q + 1, :]
+        high = corner[1, q : q + 1, :]
+        ext[pl.ds(start - 8, 8), :] = jnp.broadcast_to(jnp.where(sided[0], low, jnp.zeros_like(low)), (8, 128))
+        ext[pl.ds(start + Y, 8), :] = jnp.broadcast_to(jnp.where(sided[1], high, jnp.zeros_like(high)), (8, 128))
+
+
+def operand(values, low):
+    zero = jnp.zeros_like(values[0])
+    padded = [zero] + values + [zero]
+    return [
+        (padded[q + 1].astype(BF16), jnp.where(low, padded[q + 2], padded[q]).astype(BF16))
+        for q in range(Q)
+    ]
+
+
+def conv_own(ext, wide, banded, shifted, flipped):
+    low = low_lanes(Y)
     for x in range(X):
-        put(1 + x, 0, Y + x, below)
-        put(1 + x, YE - 1, Y + X + x, above)
-    put(0, 0, 2 * X + Y, front & below)
-    put(XE - 1, 0, 2 * X + Y, back & below)
-    put(0, YE - 1, 2 * X + Y + 1, front & above)
-    put(XE - 1, YE - 1, 2 * X + Y + 1, back & above)
-
-
-def spread(ext, wide):
+        for dy in range(3):
+            values = [ext[pl.ds(row(q, x + 1, dy - 1), Y), :] for q in range(Q)]
+            for q, (own, mixed) in enumerate(operand(values, low)):
+                wide[q, x * Y : x * Y + Y, dy * 256 : dy * 256 + 128] = own
+                wide[q, x * Y : x * Y + Y, dy * 256 + 128 : dy * 256 + 256] = mixed
+    dims = (((1,), (1 if flipped else 0,)), ((), ()))
+    result = lax.dot_general(
+        wide[...].reshape(Q * X * Y, 768), banded[...], dims, preferred_element_type=F32
+    )
+    shifted[:, Y : Y + X * Y, :] = result.reshape(Q, X * Y, 384)
+
+
+def conv_y(ext, banded, columns, flipped):
+    low = low_lanes(X)
+    for side, y, dy in ((0, -1, 0), (1, Y, 2)):
+        values = [ext[pl.ds(row(q, 1, y), X, stride=SLOT), :] for q in range(Q)]
+        padded = [jnp.zeros((X, 128), F32)] + values + [jnp.zeros((X, 128), F32)]
+        own = jnp.concatenate(values, axis=0)
+        mixed = jnp.concatenate([jnp.where(low, padded[q + 2], padded[q]) for q in range(Q)], axis=0)
+        rows = jnp.concatenate([own, mixed], axis=1).astype(BF16)
+        if flipped:
+            weight = banded[:, dy * 256 : dy * 256 + 256]
+        else:
+            weight = banded[dy * 256 : dy * 256 + 256, :]
+        dims = (((1,), (1 if flipped else 0,)), ((), ()))
+        result = lax.dot_general(rows, weight, dims, preferred_element_type=F32)
+        for q in range(Q):
+            columns[side, q, 8:16, :] = result[q * X : q * X + X]
+
+
+def conv_x(ext, thin, banded, shifted, flipped, far):
     low = low_lanes(Y)
-    zero = jnp.zeros((Y, 128), F32)
-
-    @pl.loop(0, XE)
-    def _(x):
-        rows = pl.ds(pl.multiple_of(x * Y, Y), Y)
-        for dy in range(3):
-            base = (x * YE + dy) * Q
-            pairs = [zero] + [ext[pl.ds(base + q, Y, stride=Q), :] for q in range(Q)] + [zero]
-            for q in range(Q):
-                mixed = jnp.where(low, pairs[q + 2], pairs[q])
-                wide[q, rows, dy * 256 : dy * 256 + 128] = pairs[q + 1].astype(BF16)
-                wide[q, rows, dy * 256 + 128 : dy * 256 + 256] = mixed.astype(BF16)
+    for dy in range(3):
+        values = [
+            ext[pl.ds(pl.multiple_of(row(q, far, 0), 8) + dy - 1, Y), :] for q in range(Q)
+        ]
+        for q, (own, mixed) in enumerate(operand(values, low)):
+            thin[q * Y : q * Y + Y, dy * 256 : dy * 256 + 128] = own
+            thin[q * Y : q * Y + Y, dy * 256 + 128 : dy * 256 + 256] = mixed
+    dims = (((1,), (1 if flipped else 0,)), ((), ()))
+    result = lax.dot_general(thin[...], banded[...], dims, preferred_element_type=F32)
+    start = pl.multiple_of(far * Y, Y)
+    for q in range(Q):
+        shifted[q, pl.ds(start, Y), :] = result[q * Y : q * Y + Y]
+
+
+def conv_pair(shifted, columns, sums, p):
+    n = X * Y
+    sums[...] = (
+        shifted[p, 0:n, 0:128]
+        + shifted[p, Y : Y + n, 128:256]
+        + shifted[p, 2 * Y : 2 * Y + n, 256:384]
+    )
+    for side, y in ((0, 0), (1, Y - 1)):
+        extra = (
+            columns[side, p, 7:15, 0:128]
+            + columns[side, p, 8:16, 128:256]
+            + columns[side, p, 9:17, 256:384]
+        )
+        place = pl.ds(y, X, stride=Y)
+        sums[place, :] = sums[place, :] + extra
+    return sums[...]
 
 
 TAPS = ((1, 0), (2, 1), (None, 2), (0, None))
@@ -151,30 +207,16 @@
                     banded[rows, start : start + 128] = jnp.concatenate(pieces, axis=1)
 
 
-def conv_all(wide, banded, shifted, flipped):
-    dims = (((1,), (1 if flipped else 0,)), ((), ()))
-    rows = wide[...].reshape(Q * ROWS_E, 768)
-    result = lax.dot_general(rows, banded[...], dims, preferred_element_type=F32)
-    shifted[...] = result.reshape(Q, ROWS_E, 384)
-
-
-def conv_pair(shifted, p):
-    n = X * Y
-    return (
-        shifted[p, 0:n, 0:128]
-        + shifted[p, Y : Y + n, 128:256]
-        + shifted[p, 2 * Y : 2 * Y + n, 256:384]
-    )
-
-
-def kernel_grad(wide, turned, packed, g):
+def kernel_grad(ext, turned, packed, g, finished):
     low = low_lanes(192)
     turned_value = turned[...]
 
     def moving(tap):
         dx, dy = tap // 3, tap % 3
-        block = wide[:, dx * Y : dx * Y + X * Y, dy * 256 : dy * 256 + 128]
-        return block.reshape(Q * X * Y, 128)
+        blocks = [
+            ext[pl.ds(row(q, x + dx, dy - 1), Y), :].astype(BF16) for q in range(Q) for x in range(X)
+        ]
+        return jnp.concatenate(blocks, axis=0)
 
     for pair in range(PAIRS):
         first = 2 * pair
@@ -189,6 +231,7 @@
         crossed = jnp.where(low, two[0:192], one[64:256])
         total = straight + pltpu.roll(crossed, 64, 1)
         packed[g, pair * 192 : pair * 192 + 192, :] = total.astype(BF16)
+        finished(pair)
 
 
 def turn(turned, q, block):
@@ -209,10 +252,11 @@
     sizes,
     field_hbm, first_hbm, second_hbm, cotangent_hbm,
     output, full,
-    field, first, second, cotangent, load_sems, shifted,
-    ext_f, ext_c, ext_h, wide_f, wide_c, wide_h,
-    banded_1, banded_2, banded_t, turned_c, turned_p, pre,
-    sends, lands, packed, mate, part, gathered_xy, gathered_z,
+    field, first, second, cotangent, load_sems, shifted, shifted_c,
+    ext_f, ext_c, ext_h, wide, thin, columns, sums,
+    banded_1, banded_2, banded_t, turned_c, turned_p, slope,
+    send_x, send_y, send_c, land_x, land_y, land_c, corner,
+    packed, mate, part, gathered_xy, gathered_z,
     halo_send, halo_recv, mate_send, mate_recv, xy_send, xy_recv, z_send, z_recv,
     back_xy_send, back_xy_recv, share_send, share_recv,
 ):
@@ -260,72 +304,110 @@
     def _(k):
         greet((gx, along_xy(k), grp))
 
-    fields = ((field, ext_f, 0), (cotangent, ext_c, 1))
-    for source, ext, number in fields:
-        loads[number].wait()
+    place = (gx, gy, grp)
+    sided = (gy > 0, gy < ny - 1)
+    far = (XE - 1) * (1 - gx)
+    halos = [
+        halo_copies(
+            tuple(end.at[number] for end in (send_x, send_y, send_c, land_x, land_y, land_c)),
+            halo_send.at[number], halo_recv.at[number], place, ny,
+        )
+        for number in range(3)
+    ]
+
+    def dispatch(number, ext):
+        take_edges(ext, send_x.at[number], send_y.at[number], send_c.at[number], corner, gx)
+        if number == 0:
+            pl.semaphore_wait(barrier, nz - 1 + ny - 1 + 3)
+        for copy in halos[number]:
+            copy.start()
+
+    def arrive(number, ext, then_y, then_x):
+        for which in (1, 2):
+            halos[number][which].wait_recv()
+        insert_y(ext, land_y.at[number], sided)
+        then_y()
+        for which in (0, 3, 4):
+            halos[number][which].wait_recv()
+        insert_x(ext, land_x.at[number], land_c.at[number], sided, far, corner)
+        then_x()
+
+    def load_own(ext, source):
         for x in range(X):
             for q in range(Q):
-                fill_own(ext, x, q, source[0, x, :, q * 128 : q * 128 + 128].astype(F32))
-        edge_cells(ext, sends.at[number], gx)
-    pl.semaphore_wait(barrier, nz - 1 + ny - 1 + 3)
-    for number in range(2):
-        halo_copies(
-            sends.at[number], lands.at[number], halo_send.at[number], halo_recv.at[number], gx, gy, grp, ny
-        )
+                ext[pl.ds(row(q, x + 1, 0), Y), :] = source[0, x, :, q * 128 : q * 128 + 128].astype(F32)
+
+    clear_halo(ext_f, shifted)
+    loads[0].wait()
+    load_own(ext_f, field)
+    dispatch(0, ext_f)
+    clear_halo(ext_c, shifted_c)
+    loads[1].wait()
+    load_own(ext_c, cotangent)
+    dispatch(1, ext_c)
 
     loads[2].wait()
+    forward_weight(first, banded_1)
+    conv_own(ext_f, wide, banded_1, shifted, False)
+    columns[...] = jnp.zeros_like(columns)
     loads[3].wait()
-    forward_weight(first, banded_1)
-    forward_weight(second, banded_2)
     backward_weight(second, banded_t)
     for q in range(Q):
         turn(turned_c, q, cotangent[0, :, :, q * 128 : q * 128 + 128].reshape(X * Y, 128))
 
-    halo_arrived(lands.at[0], halo_send.at[0], halo_recv.at[0], me)
-    insert_halo(ext_f, lands.at[0], gx, gy, ny)
-    spread(ext_f, wide_f)
-
-    conv_all(wide_f, banded_1, shifted, False)
-
-    @pl.loop(0, Q)
-    def _(p):
-        value = conv_pair(shifted, p)
-        pre[p] = value
-        hidden = (value * jax.nn.sigmoid(value)).astype(BF16).astype(F32)
+    arrive(
+        0, ext_f,
+        lambda: conv_y(ext_f, banded_1, columns, False),
+        lambda: conv_x(ext_f, thin, banded_1, shifted, False, far),
+    )
+
+    for p in range(Q):
+        value = conv_pair(shifted, columns, sums, p)
+        sigma = jax.nn.sigmoid(value)
+        hidden = (value * sigma).astype(BF16).astype(F32)
+        slope[p] = sigma * (1.0 + value * (1.0 - sigma))
         for x in range(X):
-            fill_own(ext_h, x, p, hidden[x * Y : x * Y + Y])
-
-    edge_cells(ext_h, sends.at[2], gx)
-    halo_copies(sends.at[2], lands.at[2], halo_send.at[2], halo_recv.at[2], gx, gy, grp, ny)
-
-    halo_arrived(lands.at[1], halo_send.at[1], halo_recv.at[1], me)
-    insert_halo(ext_c, lands.at[1], gx, gy, ny)
-    spread(ext_c, wide_c)
-    conv_all(wide_c, banded_t, shifted, True)
+            ext_h[pl.ds(row(p, x + 1, 0), Y), :] = hidden[x * Y : x * Y + Y]
+    dispatch(2, ext_h)
+    clear_halo(ext_h, shifted)
+
+    conv_own(ext_c, wide, banded_t, shifted_c, True)
+    arrive(
+        1, ext_c,
+        lambda: conv_y(ext_c, banded_t, columns, True),
+        lambda: conv_x(ext_c, thin, banded_t, shifted_c, True, far),
+    )
     for p in range(Q):
-        hidden_grad = conv_pair(shifted, p)
-        value = pre[p]
-        sigma = jax.nn.sigmoid(value)
-        turn(turned_p, p, (hidden_grad * sigma * (1.0 + value * (1.0 - sigma))).astype(BF16))
+        hidden_grad = conv_pair(shifted_c, columns, sums, p)
+        turn(turned_p, p, (hidden_grad * slope[p]).astype(BF16))
     if packed.shape[1] > PACKED:
         rest = packed.shape[1] - PACKED
-        for g in range(2):
-            packed[g, PACKED:, :] = jnp.zeros((rest, 128), BF16)
-    kernel_grad(wide_f, turned_p, packed, 0)
-
-    halo_arrived(lands.at[2], halo_send.at[2], halo_recv.at[2], me)
-    insert_halo(ext_h, lands.at[2], gx, gy, ny)
-    spread(ext_h, wide_h)
-    kernel_grad(wide_h, turned_c, packed, 1)
-
-    pair_copy = pltpu.make_async_remote_copy(
-        src_ref=packed.at[1 - core], dst_ref=mate, send_sem=mate_send, recv_sem=mate_recv,
-        device_id=sibling, device_id_type=MESH,
-    )
-    pair_copy.start()
-    pair_copy.wait_recv()
-    part[...] = (packed[core].astype(F32) + mate[...].astype(F32)).astype(BF16)
-
+        part[PACKED:, :] = jnp.zeros((rest, 128), BF16)
+
+    def mate_copy(g, pair):
+        block = pl.ds(pair * 192, 192)
+        return pltpu.make_async_remote_copy(
+            src_ref=packed.at[g, block], dst_ref=mate.at[block],
+            send_sem=mate_send.at[pair], recv_sem=mate_recv.at[pair],
+            device_id=sibling, device_id_type=MESH,
+        )
+
+    def hand_over(g):
+        def finished(pair):
+            @pl.when(core == 1 - g)
+            def _():
+                mate_copy(g, pair).start()
+
+        return finished
+
+    kernel_grad(ext_f, turned_p, packed, 0, hand_over(0))
+    forward_weight(second, banded_2)
+    arrive(2, ext_h, lambda: None, lambda: None)
+    kernel_grad(ext_h, turned_c, packed, 1, hand_over(1))
+    for pair in range(PAIRS):
+        mate_copy(0, pair).wait_recv()
+        block = pl.ds(pair * 192, 192)
+        part[block, :] = (packed[core, block, :].astype(F32) + mate[block, :].astype(F32)).astype(BF16)
     @pl.loop(1, ny)
     def _(k):
         to = along_xy(k)
@@ -336,13 +418,17 @@
             device_id=(gx, to, grp), device_id_type=MESH,
         ).start()
 
-    conv_all(wide_h, banded_2, shifted, False)
-
-    @pl.loop(0, Q)
-    def _(p):
-        value = conv_pair(shifted, p).astype(BF16)
-        columns = pl.ds(pl.multiple_of(p * 128, 128), 128)
-        output[0, :, :, columns] = value.reshape(X, Y, 128)
+    clear = jnp.zeros((8, 128), F32)
+    conv_y(ext_h, banded_2, columns, False)
+    conv_x(ext_h, thin, banded_2, shifted, False, far)
+    for q in range(Q):
+        for x in range(X):
+            ext_h[pl.ds(row(q, x + 1, -8), 8), :] = clear
+            ext_h[pl.ds(row(q, x + 1, Y), 8), :] = clear
+    conv_own(ext_h, wide, banded_2, shifted, False)
+    for p in range(Q):
+        value = conv_pair(shifted, columns, sums, p).astype(BF16)
+        output[0, :, :, p * 128 : p * 128 + 128] = value.reshape(X, Y, 128)
 
     xy_all = pltpu.make_async_remote_copy(
         src_ref=gathered_xy, dst_ref=gathered_xy, send_sem=xy_send, recv_sem=xy_recv,
@@ -411,8 +497,10 @@
     whole.wait_recv()
 
     for number in range(3):
-        halo_sent(sends.at[number], halo_send.at[number], me)
-    pair_copy.wait_send()
+        for copy in halos[number]:
+            copy.wait_send()
+    for pair in range(PAIRS):
+        mate_copy(0, pair).wait_send()
     xy_all.wait_send()
     z_all.wait_send()
     pltpu.make_async_remote_copy(
@@ -460,8 +548,8 @@
     vmem = pltpu.VMEM
     inside = pl.BlockSpec(memory_space=pltpu.VMEM)
     outside = pl.BlockSpec(memory_space=pltpu.HBM)
-    cells = (XE * YE * Q, 128)
-    wide = (Q, ROWS_E, 768)
+    cells = (Q * XE * SLOT, 128)
+    sums = (Q, ROWS_E, 384)
     weight = (27, C, C)
     output, full = pl.pallas_call(
         functools.partial(step, sizes),
@@ -473,16 +561,18 @@
         out_specs=(inside,) * 2,
         scratch_shapes=[
             vmem(field_in.shape, BF16), vmem(weight, BF16), vmem(weight, BF16), vmem(field_in.shape, BF16),
-            dma((4,)), vmem((Q, ROWS_E, 384), F32),
+            dma((4,)), vmem(sums, F32), vmem(sums, F32),
             vmem(cells, F32), vmem(cells, F32), vmem(cells, F32),
-            vmem(wide, BF16), vmem(wide, BF16), vmem(wide, BF16),
+            vmem((Q, X * Y, 768), BF16), vmem((Q * Y, 768), BF16), vmem((2, Q, 24, 384), F32), vmem((X * Y, 128), F32),
             vmem((768, 384), BF16), vmem((768, 384), BF16), vmem((384, 768), BF16),
             vmem((256, Q * 128), BF16), vmem((256, Q * 128), BF16),
             vmem((Q, X * Y, 128), F32),
-            vmem((3, 2 * X + Y, Q, 128), BF16), vmem((3, CELLS, Q, 128), BF16),
+            vmem((3, Y, 1024), BF16), vmem((3, 2, X, 1024), BF16), vmem((3, 2, Q, 128), BF16),
+            vmem((3, Y, 1024), BF16), vmem((3, 2, X, 1024), BF16), vmem((3, 2, Q, 128), BF16),
+            vmem((2, Q, 128), F32),
             vmem((2, rows, 128), BF16), vmem((rows, 128), BF16), vmem((rows, 128), BF16),
             vmem((ny - 1, chunk, 128), BF16), vmem((nz, chunk, 128), BF16),
-            dma((3, 5)), dma((3,)), dma, dma, dma, dma, dma, dma,
+            dma((3, 5)), dma((3, 5)), dma((PAIRS,)), dma((PAIRS,)), dma, dma, dma, dma,
             dma, dma((ny,)), dma, dma,
         ],
         compiler_params=pltpu.CompilerParams(

time: 52.3 us -> 52.2 us (level)
  no operation moved by 1% of the time
where the time goes in v3:
time: 52.2 us; the launch traced here: 52.1 us
  Pallas kernels  51.5 us (99%)
  between operations  0.64 us (1%)
    pallas_call x1, Pallas kernels, shards(): pl.pallas_call(functools.partial(step, sizes), out_shape=(jax.ShapeDtypeS...  50 us
    pallas_call x1, Pallas kernels, shards(): pl.pallas_call(functools.partial(unpack, 1.0 / math.sqrt(total)), out_sha...  1.5 us

profile of v3, /device:TPU:1, one launch (start us, length us, event | category | flops | bytes accessed | tf_op | source)
XLA Modules:
  0.0 52.1 jit_solution(13023868965639828460)
XLA Ops:
  0.6 50.0 %shard_map.67 = (bf16[1,8,16,1024]{3,2,1,0:T(8,128)(2,1)S(1)}, bf16[2,1024,128]{2,1,0:T(8,128)(2,1)S(1)}) custom-call(bf16[1,8,16,1024]{3,2,1,0:T(8,128)(2,1)} %field_hbm.1, bf16[27,64,64]{2,1,0:T(8,128)(2,1)} %bitcast.4, bf16[27,64,64]{2,1,0:T(8,128)(2,1)} %bitcast.5, bf16[1,8,16,1024]{3,2,1,0:T(8,128)(2,1)} %cotangent_hbm.1), custom_call_target="tpu_custom_call" | custom-call | tf_op jit(solution)/shard_map/pallas_call | solution.py:554
  50.6 1.5 %shard_map.68 = (bf16[1,8,16,1024]{3,2,1,0:T(8,128)(2,1)}, f32[27,64,64]{2,1,0:T(8,128)}, f32[27,64,64]{2,1,0:T(8,128)}) custom-call(bf16[1,8,16,1024]{3,2,1,0:T(8,128)(2,1)S(1)} %get-tuple-element.8.output_in, bf16[2,1024,128]{2,1,0:T(8,128)(2,1)S(1)} %get-tuple-element.9.full), custom_call_target="tpu_custom_call" | custom-call | tf_op jit(solution)/shard_map/pallas_call | solution.py:592

commit v4 on v3

--- a/solution.py
+++ b/solution.py
@@ -64,11 +64,11 @@
     up = lax.rem(gy + 1, count)
     down = lax.rem(gy + count - 1, count)
     moves = (
+        (send_c.at[1], land_c.at[0], (1 - gx, up, grp)),
+        (send_c.at[0], land_c.at[1], (1 - gx, down, grp)),
         (send_x, land_x, (1 - gx, gy, grp)),
         (send_y.at[1], land_y.at[0], (gx, up, grp)),
         (send_y.at[0], land_y.at[1], (gx, down, grp)),
-        (send_c.at[1], land_c.at[0], (1 - gx, up, grp)),
-        (send_c.at[0], land_c.at[1], (1 - gx, down, grp)),
     )
     return [
         pltpu.make_async_remote_copy(
@@ -256,14 +256,15 @@
     ext_f, ext_c, ext_h, wide, thin, columns, sums,
     banded_1, banded_2, banded_t, turned_c, turned_p, slope,
     send_x, send_y, send_c, land_x, land_y, land_c, corner,
-    packed, mate, part, gathered_xy, gathered_z,
-    halo_send, halo_recv, mate_send, mate_recv, xy_send, xy_recv, z_send, z_recv,
+    packed, gathered_xy, own_sum, pass_out, pass_in, gathered_z,
+    halo_send, halo_recv, pass_send, pass_recv, xy_send, xy_recv, z_send, z_recv,
     back_xy_send, back_xy_recv, share_send, share_recv,
 ):
     nx, ny, ng = sizes
     zl = ng // 2
     nz = nx * zl
-    chunk = packed.shape[1] // ny
+    chunk = gathered_xy.shape[2]
+    owners = PACKED // chunk
     loads = [
         pltpu.make_async_copy(source, target, load_sems.at[number])
         for number, (source, target) in enumerate(
@@ -323,11 +324,11 @@
             copy.start()
 
     def arrive(number, ext, then_y, then_x):
-        for which in (1, 2):
+        for which in (3, 4):
             halos[number][which].wait_recv()
         insert_y(ext, land_y.at[number], sided)
         then_y()
-        for which in (0, 3, 4):
+        for which in (0, 1, 2):
             halos[number][which].wait_recv()
         insert_x(ext, land_x.at[number], land_c.at[number], sided, far, corner)
         then_x()
@@ -354,6 +355,8 @@
     backward_weight(second, banded_t)
     for q in range(Q):
         turn(turned_c, q, cotangent[0, :, :, q * 128 : q * 128 + 128].reshape(X * Y, 128))
+
+    conv_own(ext_c, wide, banded_t, shifted_c, True)
 
     arrive(
         0, ext_f,
@@ -371,7 +374,6 @@
     dispatch(2, ext_h)
     clear_halo(ext_h, shifted)
 
-    conv_own(ext_c, wide, banded_t, shifted_c, True)
     arrive(
         1, ext_c,
         lambda: conv_y(ext_c, banded_t, columns, True),
@@ -380,96 +382,80 @@
     for p in range(Q):
         hidden_grad = conv_pair(shifted_c, columns, sums, p)
         turn(turned_p, p, (hidden_grad * slope[p]).astype(BF16))
-    if packed.shape[1] > PACKED:
-        rest = packed.shape[1] - PACKED
-        part[PACKED:, :] = jnp.zeros((rest, 128), BF16)
-
-    def mate_copy(g, pair):
-        block = pl.ds(pair * 192, 192)
-        return pltpu.make_async_remote_copy(
-            src_ref=packed.at[g, block], dst_ref=mate.at[block],
-            send_sem=mate_send.at[pair], recv_sem=mate_recv.at[pair],
-            device_id=sibling, device_id_type=MESH,
-        )
-
-    def hand_over(g):
+
+    owner = gy < owners
+
+    def scatter(g):
         def finished(pair):
-            @pl.when(core == 1 - g)
-            def _():
-                mate_copy(g, pair).start()
+            for j in range(owners):
+                if not pair * 192 < (j + 1) * chunk <= (pair + 1) * 192:
+                    continue
+
+                @pl.when(gy != j)
+                def _():
+                    pltpu.make_async_remote_copy(
+                        src_ref=packed.at[g, pl.ds(j * chunk, chunk)], dst_ref=gathered_xy.at[g, gy],
+                        send_sem=xy_send.at[g], recv_sem=xy_recv.at[g],
+                        device_id=(gx, j, grp), device_id_type=MESH,
+                    ).start()
 
         return finished
 
-    kernel_grad(ext_f, turned_p, packed, 0, hand_over(0))
+    kernel_grad(ext_f, turned_p, packed, 0, scatter(0))
     forward_weight(second, banded_2)
+    conv_own(ext_h, wide, banded_2, shifted, False)
     arrive(2, ext_h, lambda: None, lambda: None)
-    kernel_grad(ext_h, turned_c, packed, 1, hand_over(1))
-    for pair in range(PAIRS):
-        mate_copy(0, pair).wait_recv()
-        block = pl.ds(pair * 192, 192)
-        part[block, :] = (packed[core, block, :].astype(F32) + mate[block, :].astype(F32)).astype(BF16)
-    @pl.loop(1, ny)
-    def _(k):
-        to = along_xy(k)
-        pltpu.make_async_remote_copy(
-            src_ref=part.at[pl.ds(pl.multiple_of(to * chunk, 16), chunk)],
-            dst_ref=gathered_xy.at[ny - 1 - k],
-            send_sem=xy_send, recv_sem=xy_recv,
-            device_id=(gx, to, grp), device_id_type=MESH,
-        ).start()
-
-    clear = jnp.zeros((8, 128), F32)
+    kernel_grad(ext_h, turned_c, packed, 1, scatter(1))
+
     conv_y(ext_h, banded_2, columns, False)
     conv_x(ext_h, thin, banded_2, shifted, False, far)
-    for q in range(Q):
-        for x in range(X):
-            ext_h[pl.ds(row(q, x + 1, -8), 8), :] = clear
-            ext_h[pl.ds(row(q, x + 1, Y), 8), :] = clear
-    conv_own(ext_h, wide, banded_2, shifted, False)
     for p in range(Q):
         value = conv_pair(shifted, columns, sums, p).astype(BF16)
         output[0, :, :, p * 128 : p * 128 + 128] = value.reshape(X, Y, 128)
 
-    xy_all = pltpu.make_async_remote_copy(
-        src_ref=gathered_xy, dst_ref=gathered_xy, send_sem=xy_send, recv_sem=xy_recv,
-        device_id=me, device_id_type=MESH,
-    )
-    xy_all.wait_recv()
-    total = part[pl.ds(pl.multiple_of(gy * chunk, 16), chunk), :].astype(F32)
-    for k in range(ny - 1):
-        total = total + gathered_xy[k].astype(F32)
-    gathered_z[z] = total.astype(BF16)
-
-    @pl.loop(1, nz)
-    def _(k):
-        pltpu.make_async_remote_copy(
-            src_ref=gathered_z.at[z], dst_ref=gathered_z.at[z],
-            send_sem=z_send, recv_sem=z_recv,
-            device_id=z_device(along_z(k)), device_id_type=MESH,
-        ).start()
-
-    others = gathered_z.at[pl.ds(0, nz - 1)]
-    z_all = pltpu.make_async_remote_copy(
-        src_ref=others, dst_ref=others, send_sem=z_send, recv_sem=z_recv,
-        device_id=me, device_id_type=MESH,
-    )
-    z_all.wait_recv()
-    grand = gathered_z[0].astype(F32)
-    for k in range(1, nz):
-        grand = grand + gathered_z[k].astype(F32)
-
     def rows_of(j):
         return pl.ds(pl.multiple_of(j * chunk, 16), chunk)
 
-    full[core, rows_of(gy), :] = grand.astype(BF16)
-
-    @pl.loop(1, ny)
-    def _(k):
-        pltpu.make_async_remote_copy(
-            src_ref=full.at[core, rows_of(gy)], dst_ref=full.at[core, rows_of(gy)],
-            send_sem=back_xy_send, recv_sem=back_xy_recv.at[k],
-            device_id=(gx, along_xy(k), grp), device_id_type=MESH,
-        ).start()
+    def several(g, count):
+        part = gathered_xy.at[g, pl.ds(0, count)]
+        return pltpu.make_async_remote_copy(
+            src_ref=part, dst_ref=part, send_sem=xy_send.at[g], recv_sem=xy_recv.at[g],
+            device_id=me, device_id_type=MESH,
+        )
+
+    pass_on = pltpu.make_async_remote_copy(
+        src_ref=pass_out, dst_ref=pass_in, send_sem=pass_send, recv_sem=pass_recv,
+        device_id=sibling, device_id_type=MESH,
+    )
+
+    for g in range(2):
+
+        @pl.when(owner)
+        def _():
+            several(g, ny - 1).wait_recv()
+            gathered_xy[g, gy] = packed[g, rows_of(gy), :]
+            total = gathered_xy[g, 0].astype(F32)
+            for k in range(1, ny):
+                total = total + gathered_xy[g, k].astype(F32)
+
+            @pl.when(core == 1 - g)
+            def _():
+                pass_out[...] = total
+                pass_on.start()
+
+            @pl.when(core == g)
+            def _():
+                own_sum[...] = total
+                pass_on.wait_recv()
+                gathered_z[z] = (own_sum[...] + pass_in[...]).astype(BF16)
+
+                @pl.loop(1, nz)
+                def _(k):
+                    pltpu.make_async_remote_copy(
+                        src_ref=gathered_z.at[z], dst_ref=gathered_z.at[z],
+                        send_sem=z_send, recv_sem=z_recv,
+                        device_id=z_device(along_z(k)), device_id_type=MESH,
+                    ).start()
 
     def share(j):
         pltpu.make_async_remote_copy(
@@ -478,17 +464,42 @@
             device_id=sibling, device_id_type=MESH,
         ).start()
 
-    share(gy)
+    others = gathered_z.at[pl.ds(0, nz - 1)]
+    z_all = pltpu.make_async_remote_copy(
+        src_ref=others, dst_ref=others, send_sem=z_send, recv_sem=z_recv,
+        device_id=me, device_id_type=MESH,
+    )
+
+    @pl.when(owner)
+    def _():
+        z_all.wait_recv()
+        grand = gathered_z[0].astype(F32)
+        for k in range(1, nz):
+            grand = grand + gathered_z[k].astype(F32)
+        full[core, rows_of(gy), :] = grand.astype(BF16)
+
+        @pl.loop(1, ny)
+        def _(k):
+            pltpu.make_async_remote_copy(
+                src_ref=full.at[core, rows_of(gy)], dst_ref=full.at[core, rows_of(gy)],
+                send_sem=back_xy_send, recv_sem=back_xy_recv.at[k],
+                device_id=(gx, along_xy(k), grp), device_id_type=MESH,
+            ).start()
+
+        share(gy)
 
     @pl.loop(1, ny)
     def _(k):
         j = along_xy(ny - k)
-        pltpu.make_async_remote_copy(
-            src_ref=full.at[core, rows_of(j)], dst_ref=full.at[core, rows_of(j)],
-            send_sem=back_xy_send, recv_sem=back_xy_recv.at[k],
-            device_id=me, device_id_type=MESH,
-        ).wait_recv()
-        share(j)
+
+        @pl.when(j < owners)
+        def _():
+            pltpu.make_async_remote_copy(
+                src_ref=full.at[core, rows_of(j)], dst_ref=full.at[core, rows_of(j)],
+                send_sem=back_xy_send, recv_sem=back_xy_recv.at[k],
+                device_id=me, device_id_type=MESH,
+            ).wait_recv()
+            share(j)
 
     whole = pltpu.make_async_remote_copy(
         src_ref=full.at[core], dst_ref=full.at[1 - core], send_sem=share_send, recv_sem=share_recv,
@@ -499,14 +510,26 @@
     for number in range(3):
         for copy in halos[number]:
             copy.wait_send()
-    for pair in range(PAIRS):
-        mate_copy(0, pair).wait_send()
-    xy_all.wait_send()
-    z_all.wait_send()
-    pltpu.make_async_remote_copy(
-        src_ref=gathered_xy, dst_ref=gathered_xy, send_sem=back_xy_send, recv_sem=xy_recv,
-        device_id=me, device_id_type=MESH,
-    ).wait_send()
+
+    @pl.when(owner)
+    def _():
+        for g in range(2):
+            several(g, owners - 1).wait_send()
+        pass_on.wait_send()
+        z_all.wait_send()
+        pltpu.make_async_remote_copy(
+            src_ref=gathered_xy.at[0, pl.ds(0, ny - 1)], dst_ref=gathered_xy.at[0, pl.ds(0, ny - 1)],
+            send_sem=back_xy_send, recv_sem=share_recv,
+            device_id=me, device_id_type=MESH,
+        ).wait_send()
+
+    if owners < ny:
+
+        @pl.when(jnp.logical_not(owner))
+        def _():
+            for g in range(2):
+                several(g, owners).wait_send()
+
     whole.wait_send()
 
 
@@ -542,7 +565,8 @@
     nx, ny, ng = sizes
     nz = nx * ng // 2
     chunk = 16 * pl.cdiv(PACKED, 16 * ny)
-    rows = chunk * ny
+    assert PACKED % chunk == 0
+    rows = PACKED
     total = ng * nx * X * ny * Y * NZ
     dma = pltpu.SemaphoreType.DMA
     vmem = pltpu.VMEM
@@ -570,9 +594,9 @@
             vmem((3, Y, 1024), BF16), vmem((3, 2, X, 1024), BF16), vmem((3, 2, Q, 128), BF16),
             vmem((3, Y, 1024), BF16), vmem((3, 2, X, 1024), BF16), vmem((3, 2, Q, 128), BF16),
             vmem((2, Q, 128), F32),
-            vmem((2, rows, 128), BF16), vmem((rows, 128), BF16), vmem((rows, 128), BF16),
-            vmem((ny - 1, chunk, 128), BF16), vmem((nz, chunk, 128), BF16),
-            dma((3, 5)), dma((3, 5)), dma((PAIRS,)), dma((PAIRS,)), dma, dma, dma, dma,
+            vmem((2, rows, 128), BF16), vmem((2, ny, chunk, 128), BF16),
+            vmem((chunk, 128), F32), vmem((chunk, 128), F32), vmem((chunk, 128), F32), vmem((nz, chunk, 128), BF16),
+            dma((3, 5)), dma((3, 5)), dma, dma, dma((2,)), dma((2,)), dma, dma,
             dma, dma((ny,)), dma, dma,
         ],
         compiler_params=pltpu.CompilerParams(

time: 52.2 us -> 47.2 us (0.904)
  Pallas kernels: 51.5 us -> 46.5 us
    pallas_call x1, Pallas kernels: 50 us -> 45 us  [shards(): pl.pallas_call(functools.partial(step, sizes), out_shape=(jax.ShapeDtypeS...]
where the time goes in v4:
time: 47.2 us; the launch traced here: 47.1 us
  Pallas kernels  46.5 us (99%)
  between operations  0.64 us (1%)
    pallas_call x1, Pallas kernels, shards(): pl.pallas_call(functools.partial(step, sizes), out_shape=(jax.ShapeDtypeS...  45 us
    pallas_call x1, Pallas kernels, shards(): pl.pallas_call(functools.partial(unpack, 1.0 / math.sqrt(total)), out_sha...  1.51 us

profile of v4, /device:TPU:1, one launch (start us, length us, event | category | flops | bytes accessed | tf_op | source)
XLA Modules:
  0.0 47.1 jit_solution(6945587579884095091)
XLA Ops:
  0.6 45.0 %shard_map.67 = (bf16[1,8,16,1024]{3,2,1,0:T(8,128)(2,1)S(1)}, bf16[2,960,128]{2,1,0:T(8,128)(2,1)S(1)}) custom-call(bf16[1,8,16,1024]{3,2,1,0:T(8,128)(2,1)} %field_hbm.1, bf16[27,64,64]{2,1,0:T(8,128)(2,1)} %bitcast.4, bf16[27,64,64]{2,1,0:T(8,128)(2,1)} %bitcast.5, bf16[1,8,16,1024]{3,2,1,0:T(8,128)(2,1)} %cotangent_hbm.1), custom_call_target="tpu_custom_call" | custom-call | tf_op jit(solution)/shard_map/pallas_call | solution.py:578
  45.6 1.5 %shard_map.68 = (bf16[1,8,16,1024]{3,2,1,0:T(8,128)(2,1)}, f32[27,64,64]{2,1,0:T(8,128)}, f32[27,64,64]{2,1,0:T(8,128)}) custom-call(bf16[1,8,16,1024]{3,2,1,0:T(8,128)(2,1)S(1)} %get-tuple-element.8.output_in, bf16[2,960,128]{2,1,0:T(8,128)(2,1)S(1)} %get-tuple-element.9.full), custom_call_target="tpu_custom_call" | custom-call | tf_op jit(solution)/shard_map/pallas_call | solution.py:616

commit v5 on v4

--- a/solution.py
+++ b/solution.py
@@ -476,7 +476,17 @@
         grand = gathered_z[0].astype(F32)
         for k in range(1, nz):
             grand = grand + gathered_z[k].astype(F32)
-        full[core, rows_of(gy), :] = grand.astype(BF16)
+        rows = lax.broadcasted_iota(jnp.int32, (128, 128), 0)
+        lanes = lax.broadcasted_iota(jnp.int32, (128, 128), 1)
+        unit = (rows == lanes).astype(BF16)
+        turned = []
+        for start in range(0, chunk, C):
+            block = lax.dot_general(
+                unit, grand[start : start + C].astype(BF16), (((1,), (1,)), ((), ())),
+                preferred_element_type=F32,
+            )
+            turned.append(jnp.concatenate([block[0:C], block[C : 2 * C]], axis=1))
+        full[core, rows_of(gy), :] = jnp.concatenate(turned, axis=0).astype(BF16)
 
         @pl.loop(1, ny)
         def _(k):
@@ -541,21 +551,14 @@
         )
     ]
     copies[0].start()
-    rows = lax.broadcasted_iota(jnp.int32, (128, 128), 0)
-    lanes = lax.broadcasted_iota(jnp.int32, (128, 128), 1)
-    unit = (rows == lanes).astype(BF16)
     for g, target in ((0, one), (1, two)):
         for pair in range(PAIRS):
             for v in range(3):
-                start = pair * 192 + v * 64
-                block = lax.dot_general(
-                    unit, full[g, start : start + 64, :], (((1,), (1,)), ((), ())),
-                    preferred_element_type=F32,
-                ) * factor
-                for half in range(2):
-                    tap = 2 * pair + half
-                    if tap < 9:
-                        target[tap * 3 + 2 - v] = block[half * 64 : half * 64 + 64]
+                start = (pair * 3 + v) * C
+                block = full[g, start : start + C, :].astype(F32) * factor
+                target[2 * pair * 3 + 2 - v] = block[:, 0:C]
+                if 2 * pair + 1 < 9:
+                    target[(2 * pair + 1) * 3 + 2 - v] = block[:, C : 2 * C]
         copies[g + 1].start()
     for copy in copies:
         copy.wait()
@@ -564,7 +567,7 @@
 def shards(sizes, field_in, first_weight, second_weight, cotangent):
     nx, ny, ng = sizes
     nz = nx * ng // 2
-    chunk = 16 * pl.cdiv(PACKED, 16 * ny)
+    chunk = C * pl.cdiv(PACKED, C * ny)
     assert PACKED % chunk == 0
     rows = PACKED
     total = ng * nx * X * ny * Y * NZ

time: 47.2 us -> 47.1 us (level)
  no operation moved by 1% of the time
where the time goes in v5:
time: 47.1 us; the launch traced here: 47 us
  Pallas kernels  46.4 us (99%)
  between operations  0.64 us (1%)
    pallas_call x1, Pallas kernels, shards(): pl.pallas_call(functools.partial(step, sizes), out_shape=(jax.ShapeDtypeS...  45 us
    pallas_call x1, Pallas kernels, shards(): pl.pallas_call(functools.partial(unpack, 1.0 / math.sqrt(total)), out_sha...  1.44 us

profile of v5, /device:TPU:1, one launch (start us, length us, event | category | flops | bytes accessed | tf_op | source)
XLA Modules:
  0.0 47.0 jit_solution(11332283459381603956)
XLA Ops:
  0.6 45.0 %shard_map.67 = (bf16[1,8,16,1024]{3,2,1,0:T(8,128)(2,1)S(1)}, bf16[2,960,128]{2,1,0:T(8,128)(2,1)S(1)}) custom-call(bf16[1,8,16,1024]{3,2,1,0:T(8,128)(2,1)} %field_hbm.1, bf16[27,64,64]{2,1,0:T(8,128)(2,1)} %bitcast.4, bf16[27,64,64]{2,1,0:T(8,128)(2,1)} %bitcast.5, bf16[1,8,16,1024]{3,2,1,0:T(8,128)(2,1)} %cotangent_hbm.1), custom_call_target="tpu_custom_call" | custom-call | tf_op jit(solution)/shard_map/pallas_call | solution.py:581
  45.6 1.4 %shard_map.68 = (bf16[1,8,16,1024]{3,2,1,0:T(8,128)(2,1)}, f32[27,64,64]{2,1,0:T(8,128)}, f32[27,64,64]{2,1,0:T(8,128)}) custom-call(bf16[1,8,16,1024]{3,2,1,0:T(8,128)(2,1)S(1)} %get-tuple-element.8.output_in, bf16[2,960,128]{2,1,0:T(8,128)(2,1)S(1)} %get-tuple-element.9.full), custom_call_target="tpu_custom_call" | custom-call | tf_op jit(solution)/shard_map/pallas_call | solution.py:619

commit v6 on v5

--- a/solution.py
+++ b/solution.py
@@ -14,7 +14,10 @@
 Y = 16
 Q = 8
 XE = X + 2
+PLANES = 16
+FAR = 10
 SLOT = 32
+MARGIN = 8
 ROWS_E = XE * Y
 PAIRS = 5
 PACKED = PAIRS * 192
@@ -28,7 +31,7 @@
 
 
 def row(q, x, y):
-    return (q * XE + x) * SLOT + 8 + y
+    return (q * PLANES + x) * SLOT + MARGIN + 8 + y
 
 
 def clear_halo(ext, shifted):
@@ -41,20 +44,25 @@
             else:
                 ext[pl.ds(row(q, x, -8), 8), :] = edge
                 ext[pl.ds(row(q, x, Y), 8), :] = edge
-        shifted[q, 0:Y, :] = jnp.zeros((Y, 384), F32)
-        shifted[q, ROWS_E - Y : ROWS_E, :] = jnp.zeros((Y, 384), F32)
+        if shifted is not None:
+            shifted[q, 0:Y, :] = jnp.zeros((Y, 384), F32)
+            shifted[q, ROWS_E - Y : ROWS_E, :] = jnp.zeros((Y, 384), F32)
 
 
 def take_edges(ext, send_x, send_y, send_c, corner, gx):
-    near = X - (X - 1) * gx
+    deep = send_x.shape[0]
     for q in range(Q):
         columns = slice(q * 128, q * 128 + 128)
-        plane = ext[pl.ds(pl.multiple_of(row(q, near, 0), 8), Y), :]
-        send_x[:, columns] = plane.astype(BF16)
-        corner[0, q : q + 1, :] = plane[0:1]
-        corner[1, q : q + 1, :] = plane[Y - 1 : Y]
-        for side, y in ((0, 0), (1, Y - 1)):
-            send_y[side, :, columns] = ext[pl.ds(row(q, 1, y), X, stride=SLOT), :].astype(BF16)
+        for d in range(deep):
+            near = (X - d) - (X - 1 - 2 * d) * gx
+            plane = ext[pl.ds(pl.multiple_of(row(q, near, 0), 8), Y), :]
+            send_x[d, :, columns] = plane.astype(BF16)
+            for e in range(deep):
+                corner[0, d * deep + e, q : q + 1, :] = plane[e : e + 1]
+                corner[1, d * deep + e, q : q + 1, :] = plane[Y - 1 - e : Y - e]
+        for e in range(deep):
+            for side, y in ((0, e), (1, Y - 1 - e)):
+                send_y[side, e, :, columns] = ext[pl.ds(row(q, 1, y), X, stride=SLOT), :].astype(BF16)
     send_c[...] = corner[...].astype(BF16)
 
 
@@ -80,22 +88,31 @@
 
 
 def insert_y(ext, land_y, sided):
-    for side, y in ((0, -1), (1, Y)):
+    for e in range(land_y.shape[1]):
+        for side, y in ((0, -1 - e), (1, Y + e)):
+            for q in range(Q):
+                value = land_y[side, e, :, q * 128 : q * 128 + 128].astype(F32)
+                value = jnp.where(sided[side], value, jnp.zeros_like(value))
+                ext[pl.ds(row(q, 1, y), X, stride=SLOT), :] = value
+
+
+def insert_x(ext, land_x, land_c, sided, far, corner):
+    deep = land_x.shape[0]
+    corner[...] = land_c[...].astype(F32)
+    rows = lax.broadcasted_iota(jnp.int32, (8, 128), 0)
+    for d in range(deep):
+        plane = far if d == 0 else FAR
         for q in range(Q):
-            value = land_y[side, :, q * 128 : q * 128 + 128].astype(F32)
-            value = jnp.where(sided[side], value, jnp.zeros_like(value))
-            ext[pl.ds(row(q, 1, y), X, stride=SLOT), :] = value
-
-
-def insert_x(ext, land_x, land_c, sided, far, corner):
-    corner[...] = land_c[...].astype(F32)
-    for q in range(Q):
-        start = pl.multiple_of(row(q, far, 0), 8)
-        ext[pl.ds(start, Y), :] = land_x[:, q * 128 : q * 128 + 128].astype(F32)
-        low = corner[0, q : q + 1, :]
-        high = corner[1, q : q + 1, :]
-        ext[pl.ds(start - 8, 8), :] = jnp.broadcast_to(jnp.where(sided[0], low, jnp.zeros_like(low)), (8, 128))
-        ext[pl.ds(start + Y, 8), :] = jnp.broadcast_to(jnp.where(sided[1], high, jnp.zeros_like(high)), (8, 128))
+            start = pl.multiple_of(row(q, plane, 0), 8)
+            ext[pl.ds(start, Y), :] = land_x[d, :, q * 128 : q * 128 + 128].astype(F32)
+            low = jnp.zeros((8, 128), F32)
+            high = jnp.zeros((8, 128), F32)
+            for e in range(deep):
+                cell = d * deep + e
+                low = jnp.where((rows == 7 - e) & sided[0], corner[0, cell, q : q + 1, :], low)
+                high = jnp.where((rows == e) & sided[1], corner[1, cell, q : q + 1, :], high)
+            ext[pl.ds(start - 8, 8), :] = low
+            ext[pl.ds(start + Y, 8), :] = high
 
 
 def operand(values, low):
@@ -156,13 +173,69 @@
         shifted[q, pl.ds(start, Y), :] = result[q * Y : q * Y + Y]
 
 
-def conv_pair(shifted, columns, sums, p):
+def silu(value):
+    return (value * jax.nn.sigmoid(value)).astype(BF16).astype(F32)
+
+
+def lanes_of(values, low):
+    padded = [jnp.zeros_like(values[0])] + values + [jnp.zeros_like(values[0])]
+    own = jnp.concatenate(values, axis=0)
+    mixed = jnp.concatenate([jnp.where(low, padded[q + 2], padded[q]) for q in range(Q)], axis=0)
+    return [own.astype(BF16), mixed.astype(BF16)]
+
+
+def ring_x(ext, hidden_ext, banded, sided, gx, far):
+    low = low_lanes(SLOT)
+    total = jnp.zeros((Q * SLOT, 128), F32)
+    for dx, plane in enumerate((X + 2 * gx, far, FAR - (XE - 1) * gx)):
+        parts = []
+        for dy in range(3):
+            starts = [pl.multiple_of(row(q, plane, -8), 8) + dy - 1 for q in range(Q)]
+            parts += lanes_of([ext[pl.ds(start, SLOT), :] for start in starts], low)
+        total = total + jnp.dot(
+            jnp.concatenate(parts, axis=1), banded[:, dx * 128 : dx * 128 + 128], preferred_element_type=F32
+        )
+    hidden = silu(total)
+    y = lax.broadcasted_iota(jnp.int32, (SLOT, 128), 0) - 8
+    inside = ((y >= 0) & (y < Y)) | ((y == -1) & sided[0]) | ((y == Y) & sided[1])
+    for q in range(Q):
+        part = hidden[q * SLOT : q * SLOT + SLOT]
+        hidden_ext[pl.ds(pl.multiple_of(row(q, far, -8), 8), SLOT), :] = jnp.where(inside, part, jnp.zeros_like(part))
+
+
+def ring_y(ext, hidden_ext, banded, ring, sided):
+    low = low_lanes(PLANES)
+    for side, y in ((0, -1), (1, Y)):
+        parts = []
+        for dy in range(3):
+            parts += lanes_of(
+                [ext[pl.ds(row(q, 0, y + dy - 1), PLANES, stride=SLOT), :] for q in range(Q)], low
+            )
+        ring[...] = jnp.dot(jnp.concatenate(parts, axis=1), banded[...], preferred_element_type=F32)
+        for q in range(Q):
+            start = q * PLANES
+            total = (
+                ring[start : start + X, 0:128]
+                + ring[start + 1 : start + 1 + X, 128:256]
+                + ring[start + 2 : start + 2 + X, 256:384]
+            )
+            hidden = silu(total)
+            hidden_ext[pl.ds(row(q, 1, y), X, stride=SLOT), :] = jnp.where(
+                sided[side], hidden, jnp.zeros_like(hidden)
+            )
+
+
+def plane_sum(shifted, p):
     n = X * Y
-    sums[...] = (
+    return (
         shifted[p, 0:n, 0:128]
         + shifted[p, Y : Y + n, 128:256]
         + shifted[p, 2 * Y : 2 * Y + n, 256:384]
     )
+
+
+def conv_pair(shifted, columns, sums, p):
+    sums[...] = plane_sum(shifted, p)
     for side, y in ((0, 0), (1, Y - 1)):
         extra = (
             columns[side, p, 7:15, 0:128]
@@ -255,7 +328,8 @@
     field, first, second, cotangent, load_sems, shifted, shifted_c,
     ext_f, ext_c, ext_h, wide, thin, columns, sums,
     banded_1, banded_2, banded_t, turned_c, turned_p, slope,
-    send_x, send_y, send_c, land_x, land_y, land_c, corner,
+    send_xf, send_yf, send_cf, land_xf, land_yf, land_cf, corner_f,
+    send_xc, send_yc, send_cc, land_xc, land_yc, land_cc, corner_c, ring,
     packed, gathered_xy, own_sum, pass_out, pass_in, gathered_z,
     halo_send, halo_recv, pass_send, pass_recv, xy_send, xy_recv, z_send, z_recv,
     back_xy_send, back_xy_recv, share_send, share_recv,
@@ -308,29 +382,32 @@
     place = (gx, gy, grp)
     sided = (gy > 0, gy < ny - 1)
     far = (XE - 1) * (1 - gx)
+    ends = (
+        (send_xf, send_yf, send_cf, land_xf, land_yf, land_cf),
+        (send_xc, send_yc, send_cc, land_xc, land_yc, land_cc),
+    )
+    corners = (corner_f, corner_c)
     halos = [
-        halo_copies(
-            tuple(end.at[number] for end in (send_x, send_y, send_c, land_x, land_y, land_c)),
-            halo_send.at[number], halo_recv.at[number], place, ny,
-        )
-        for number in range(3)
+        halo_copies(ends[number], halo_send.at[number], halo_recv.at[number], place, ny)
+        for number in range(2)
     ]
 
     def dispatch(number, ext):
-        take_edges(ext, send_x.at[number], send_y.at[number], send_c.at[number], corner, gx)
+        take_edges(ext, *ends[number][:3], corners[number], gx)
         if number == 0:
             pl.semaphore_wait(barrier, nz - 1 + ny - 1 + 3)
         for copy in halos[number]:
             copy.start()
 
     def arrive(number, ext, then_y, then_x):
+        land_x, land_y, land_c = ends[number][3:]
         for which in (3, 4):
             halos[number][which].wait_recv()
-        insert_y(ext, land_y.at[number], sided)
+        insert_y(ext, land_y, sided)
         then_y()
         for which in (0, 1, 2):
             halos[number][which].wait_recv()
-        insert_x(ext, land_x.at[number], land_c.at[number], sided, far, corner)
+        insert_x(ext, land_x, land_c, sided, far, corners[number])
         then_x()
 
     def load_own(ext, source):
@@ -357,6 +434,8 @@
         turn(turned_c, q, cotangent[0, :, :, q * 128 : q * 128 + 128].reshape(X * Y, 128))
 
     conv_own(ext_c, wide, banded_t, shifted_c, True)
+    forward_weight(second, banded_2)
+    clear_halo(ext_h, None)
 
     arrive(
         0, ext_f,
@@ -371,17 +450,8 @@
         slope[p] = sigma * (1.0 + value * (1.0 - sigma))
         for x in range(X):
             ext_h[pl.ds(row(p, x + 1, 0), Y), :] = hidden[x * Y : x * Y + Y]
-    dispatch(2, ext_h)
-    clear_halo(ext_h, shifted)
-
-    arrive(
-        1, ext_c,
-        lambda: conv_y(ext_c, banded_t, columns, True),
-        lambda: conv_x(ext_c, thin, banded_t, shifted_c, True, far),
-    )
-    for p in range(Q):
-        hidden_grad = conv_pair(shifted_c, columns, sums, p)
-        turn(turned_p, p, (hidden_grad * slope[p]).astype(BF16))
+    ring_x(ext_f, ext_h, banded_1, sided, gx, far)
+    ring_y(ext_f, ext_h, banded_1, ring, sided)
 
     owner = gy < owners
 
@@ -401,16 +471,21 @@
 
         return finished
 
+    kernel_grad(ext_h, turned_c, packed, 1, scatter(1))
+    arrive(
+        1, ext_c,
+        lambda: conv_y(ext_c, banded_t, columns, True),
+        lambda: conv_x(ext_c, thin, banded_t, shifted_c, True, far),
+    )
+    for p in range(Q):
+        hidden_grad = conv_pair(shifted_c, columns, sums, p)
+        turn(turned_p, p, (hidden_grad * slope[p]).astype(BF16))
     kernel_grad(ext_f, turned_p, packed, 0, scatter(0))
-    forward_weight(second, banded_2)
+
     conv_own(ext_h, wide, banded_2, shifted, False)
-    arrive(2, ext_h, lambda: None, lambda: None)
-    kernel_grad(ext_h, turned_c, packed, 1, scatter(1))
-
-    conv_y(ext_h, banded_2, columns, False)
     conv_x(ext_h, thin, banded_2, shifted, False, far)
     for p in range(Q):
-        value = conv_pair(shifted, columns, sums, p).astype(BF16)
+        value = plane_sum(shifted, p).astype(BF16)
         output[0, :, :, p * 128 : p * 128 + 128] = value.reshape(X, Y, 128)
 
     def rows_of(j):
@@ -428,7 +503,7 @@
         device_id=sibling, device_id_type=MESH,
     )
 
-    for g in range(2):
+    for g in (1, 0):
 
         @pl.when(owner)
         def _():
@@ -517,7 +592,7 @@
     )
     whole.wait_recv()
 
-    for number in range(3):
+    for number in range(2):
         for copy in halos[number]:
             copy.wait_send()
 
@@ -564,6 +639,15 @@
         copy.wait()
 
 
+def halo_buffers(deep):
+    ends = [
+        pltpu.VMEM((deep, Y, 1024), BF16),
+        pltpu.VMEM((2, deep, X, 1024), BF16),
+        pltpu.VMEM((2, deep * deep, Q, 128), BF16),
+    ]
+    return ends + ends + [pltpu.VMEM((2, deep * deep, Q, 128), F32)]
+
+
 def shards(sizes, field_in, first_weight, second_weight, cotangent):
     nx, ny, ng = sizes
     nz = nx * ng // 2
@@ -575,7 +659,7 @@
     vmem = pltpu.VMEM
     inside = pl.BlockSpec(memory_space=pltpu.VMEM)
     outside = pl.BlockSpec(memory_space=pltpu.HBM)
-    cells = (Q * XE * SLOT, 128)
+    cells = (Q * PLANES * SLOT + 2 * MARGIN, 128)
     sums = (Q, ROWS_E, 384)
     weight = (27, C, C)
     output, full = pl.pallas_call(
@@ -594,12 +678,10 @@
             vmem((768, 384), BF16), vmem((768, 384), BF16), vmem((384, 768), BF16),
             vmem((256, Q * 128), BF16), vmem((256, Q * 128), BF16),
             vmem((Q, X * Y, 128), F32),
-            vmem((3, Y, 1024), BF16), vmem((3, 2, X, 1024), BF16), vmem((3, 2, Q, 128), BF16),
-            vmem((3, Y, 1024), BF16), vmem((3, 2, X, 1024), BF16), vmem((3, 2, Q, 128), BF16),
-            vmem((2, Q, 128), F32),
+            *halo_buffers(2), *halo_buffers(1), vmem((Q * PLANES, 384), F32),
             vmem((2, rows, 128), BF16), vmem((2, ny, chunk, 128), BF16),
             vmem((chunk, 128), F32), vmem((chunk, 128), F32), vmem((chunk, 128), F32), vmem((nz, chunk, 128), BF16),
-            dma((3, 5)), dma((3, 5)), dma, dma, dma((2,)), dma((2,)), dma, dma,
+            dma((2, 5)), dma((2, 5)), dma, dma, dma((2,)), dma((2,)), dma, dma,
             dma, dma((ny,)), dma, dma,
         ],
         compiler_params=pltpu.CompilerParams(

time: 47.1 us -> 46.7 us (level)
  no operation moved by 1% of the time
where the time goes in v6:
time: 46.7 us; the launch traced here: 46.6 us
  Pallas kernels  46 us (99%)
  between operations  0.64 us (1%)
    pallas_call x1, Pallas kernels, shards(): pl.pallas_call(functools.partial(step, sizes), out_shape=(jax.ShapeDtypeS...  44.5 us
    pallas_call x1, Pallas kernels, shards(): pl.pallas_call(functools.partial(unpack, 1.0 / math.sqrt(total)), out_sha...  1.44 us

profile of v6, /device:TPU:1, one launch (start us, length us, event | category | flops | bytes accessed | tf_op | source)
XLA Modules:
  0.0 46.6 jit_solution(1161586615951517929)
XLA Ops:
  0.6 44.5 %shard_map.67 = (bf16[1,8,16,1024]{3,2,1,0:T(8,128)(2,1)S(1)}, bf16[2,960,128]{2,1,0:T(8,128)(2,1)S(1)}) custom-call(bf16[1,8,16,1024]{3,2,1,0:T(8,128)(2,1)} %field_hbm.1, bf16[27,64,64]{2,1,0:T(8,128)(2,1)} %bitcast.4, bf16[27,64,64]{2,1,0:T(8,128)(2,1)} %bitcast.5, bf16[1,8,16,1024]{3,2,1,0:T(8,128)(2,1)} %cotangent_hbm.1), custom_call_target="tpu_custom_call" | custom-call | tf_op jit(solution)/shard_map/pallas_call | solution.py:665
  45.2 1.4 %shard_map.68 = (bf16[1,8,16,1024]{3,2,1,0:T(8,128)(2,1)}, f32[27,64,64]{2,1,0:T(8,128)}, f32[27,64,64]{2,1,0:T(8,128)}) custom-call(bf16[1,8,16,1024]{3,2,1,0:T(8,128)(2,1)S(1)} %get-tuple-element.8.output_in, bf16[2,960,128]{2,1,0:T(8,128)(2,1)S(1)} %get-tuple-element.9.full), custom_call_target="tpu_custom_call" | custom-call | tf_op jit(solution)/shard_map/pallas_call | solution.py:701

commit v7 on v6

--- a/solution.py
+++ b/solution.py
@@ -157,7 +157,7 @@
             columns[side, q, 8:16, :] = result[q * X : q * X + X]
 
 
-def conv_x(ext, thin, banded, shifted, flipped, far):
+def conv_x(ext, thin, banded, flipped, gx, far):
     low = low_lanes(Y)
     for dy in range(3):
         values = [
@@ -166,11 +166,16 @@
         for q, (own, mixed) in enumerate(operand(values, low)):
             thin[q * Y : q * Y + Y, dy * 256 : dy * 256 + 128] = own
             thin[q * Y : q * Y + Y, dy * 256 + 128 : dy * 256 + 256] = mixed
+    tap = pl.ds(pl.multiple_of((1 - gx) * 256, 128), 128)
+    weight = banded[tap, :] if flipped else banded[:, tap]
     dims = (((1,), (1 if flipped else 0,)), ((), ()))
-    result = lax.dot_general(thin[...], banded[...], dims, preferred_element_type=F32)
-    start = pl.multiple_of(far * Y, Y)
+    return lax.dot_general(thin[...], weight, dims, preferred_element_type=F32)
+
+
+def add_plane(sums, added, gx):
+    edge = pl.ds(pl.multiple_of((X - 1) * (1 - gx) * Y, Y), Y)
     for q in range(Q):
-        shifted[q, pl.ds(start, Y), :] = result[q * Y : q * Y + Y]
+        sums[q, edge, :] = sums[q, edge, :] + added[q * Y : q * Y + Y]
 
 
 def silu(value):
@@ -234,8 +239,10 @@
     )
 
 
-def conv_pair(shifted, columns, sums, p):
-    sums[...] = plane_sum(shifted, p)
+def conv_sum(shifted, columns, sums, p):
+    sums[p] = plane_sum(shifted, p)
+    if columns is None:
+        return
     for side, y in ((0, 0), (1, Y - 1)):
         extra = (
             columns[side, p, 7:15, 0:128]
@@ -243,8 +250,7 @@
             + columns[side, p, 9:17, 256:384]
         )
         place = pl.ds(y, X, stride=Y)
-        sums[place, :] = sums[place, :] + extra
-    return sums[...]
+        sums[p, place, :] = sums[p, place, :] + extra
 
 
 TAPS = ((1, 0), (2, 1), (None, 2), (0, None))
@@ -326,7 +332,7 @@
     field_hbm, first_hbm, second_hbm, cotangent_hbm,
     output, full,
     field, first, second, cotangent, load_sems, shifted, shifted_c,
-    ext_f, ext_c, ext_h, wide, thin, columns, sums,
+    ext_f, ext_c, ext_h, wide, thin, columns, columns_c, pre, sums_c,
     banded_1, banded_2, banded_t, turned_c, turned_p, slope,
     send_xf, send_yf, send_cf, land_xf, land_yf, land_cf, corner_f,
     send_xc, send_yc, send_cc, land_xc, land_yc, land_cc, corner_c, ring,
@@ -369,13 +375,15 @@
 
     greet((1 - gx, along_xy(1), grp))
     greet((1 - gx, along_xy(ny - 1), grp))
+    greet((1 - gx, gy, grp))
+    greet((gx, along_xy(1), grp))
+    greet((gx, along_xy(ny - 1), grp))
     greet(sibling)
-
-    @pl.loop(1, nz)
-    def _(k):
-        greet(z_device(along_z(k)))
-
-    @pl.loop(1, ny)
+    for k in range(1, nz):
+        if k != zl:
+            greet(z_device(along_z(k)))
+
+    @pl.loop(2, ny - 1)
     def _(k):
         greet((gx, along_xy(k), grp))
 
@@ -399,16 +407,15 @@
         for copy in halos[number]:
             copy.start()
 
-    def arrive(number, ext, then_y, then_x):
-        land_x, land_y, land_c = ends[number][3:]
+    def arrive_y(number, ext):
         for which in (3, 4):
             halos[number][which].wait_recv()
-        insert_y(ext, land_y, sided)
-        then_y()
+        insert_y(ext, ends[number][4], sided)
+
+    def arrive_x(number, ext):
         for which in (0, 1, 2):
             halos[number][which].wait_recv()
-        insert_x(ext, land_x, land_c, sided, far, corners[number])
-        then_x()
+        insert_x(ext, ends[number][3], ends[number][5], sided, far, corners[number])
 
     def load_own(ext, source):
         for x in range(X):
@@ -428,6 +435,7 @@
     forward_weight(first, banded_1)
     conv_own(ext_f, wide, banded_1, shifted, False)
     columns[...] = jnp.zeros_like(columns)
+    columns_c[...] = jnp.zeros_like(columns_c)
     loads[3].wait()
     backward_weight(second, banded_t)
     for q in range(Q):
@@ -437,19 +445,29 @@
     forward_weight(second, banded_2)
     clear_halo(ext_h, None)
 
-    arrive(
-        0, ext_f,
-        lambda: conv_y(ext_f, banded_1, columns, False),
-        lambda: conv_x(ext_f, thin, banded_1, shifted, False, far),
-    )
-
+    def activate(value):
+        sigma = jax.nn.sigmoid(value)
+        return (value * sigma).astype(BF16).astype(F32), sigma * (1.0 + value * (1.0 - sigma))
+
+    arrive_y(0, ext_f)
+    conv_y(ext_f, banded_1, columns, False)
     for p in range(Q):
-        value = conv_pair(shifted, columns, sums, p)
-        sigma = jax.nn.sigmoid(value)
-        hidden = (value * sigma).astype(BF16).astype(F32)
-        slope[p] = sigma * (1.0 + value * (1.0 - sigma))
+        conv_sum(shifted, columns, pre, p)
+        hidden, slope[p] = activate(pre[p])
         for x in range(X):
             ext_h[pl.ds(row(p, x + 1, 0), Y), :] = hidden[x * Y : x * Y + Y]
+    arrive_y(1, ext_c)
+    conv_y(ext_c, banded_t, columns_c, True)
+    for p in range(Q):
+        conv_sum(shifted_c, columns_c, sums_c, p)
+
+    arrive_x(0, ext_f)
+    add_plane(pre, conv_x(ext_f, thin, banded_1, False, gx, far), gx)
+    edge = (X - 1) * (1 - gx)
+    edge_rows = pl.ds(pl.multiple_of(edge * Y, Y), Y)
+    for p in range(Q):
+        hidden, slope[p, edge_rows, :] = activate(pre[p, edge_rows, :])
+        ext_h[pl.ds(pl.multiple_of(row(p, edge + 1, 0), 8), Y), :] = hidden
     ring_x(ext_f, ext_h, banded_1, sided, gx, far)
     ring_y(ext_f, ext_h, banded_1, ring, sided)
 
@@ -472,21 +490,19 @@
         return finished
 
     kernel_grad(ext_h, turned_c, packed, 1, scatter(1))
-    arrive(
-        1, ext_c,
-        lambda: conv_y(ext_c, banded_t, columns, True),
-        lambda: conv_x(ext_c, thin, banded_t, shifted_c, True, far),
-    )
+    arrive_x(1, ext_c)
+    add_plane(sums_c, conv_x(ext_c, thin, banded_t, True, gx, far), gx)
     for p in range(Q):
-        hidden_grad = conv_pair(shifted_c, columns, sums, p)
-        turn(turned_p, p, (hidden_grad * slope[p]).astype(BF16))
+        turn(turned_p, p, (sums_c[p] * slope[p]).astype(BF16))
+
     kernel_grad(ext_f, turned_p, packed, 0, scatter(0))
 
     conv_own(ext_h, wide, banded_2, shifted, False)
-    conv_x(ext_h, thin, banded_2, shifted, False, far)
     for p in range(Q):
-        value = plane_sum(shifted, p).astype(BF16)
-        output[0, :, :, p * 128 : p * 128 + 128] = value.reshape(X, Y, 128)
+        conv_sum(shifted, None, pre, p)
+    add_plane(pre, conv_x(ext_h, thin, banded_2, False, gx, far), gx)
+    for p in range(Q):
+        output[0, :, :, p * 128 : p * 128 + 128] = pre[p].astype(BF16).reshape(X, Y, 128)
 
     def rows_of(j):
         return pl.ds(pl.multiple_of(j * chunk, 16), chunk)
@@ -524,8 +540,7 @@
                 pass_on.wait_recv()
                 gathered_z[z] = (own_sum[...] + pass_in[...]).astype(BF16)
 
-                @pl.loop(1, nz)
-                def _(k):
+                for k in sorted(range(1, nz), key=lambda k: -min(k, nz - k)):
                     pltpu.make_async_remote_copy(
                         src_ref=gathered_z.at[z], dst_ref=gathered_z.at[z],
                         send_sem=z_send, recv_sem=z_recv,
@@ -539,6 +554,9 @@
             device_id=sibling, device_id_type=MESH,
         ).start()
 
+    by_distance = sorted(
+        range(1, ny), key=lambda k: -(min(k // 4, 4 - k // 4) + min(k % 4, 4 - k % 4))
+    )
     others = gathered_z.at[pl.ds(0, nz - 1)]
     z_all = pltpu.make_async_remote_copy(
         src_ref=others, dst_ref=others, send_sem=z_send, recv_sem=z_recv,
@@ -563,8 +581,7 @@
             turned.append(jnp.concatenate([block[0:C], block[C : 2 * C]], axis=1))
         full[core, rows_of(gy), :] = jnp.concatenate(turned, axis=0).astype(BF16)
 
-        @pl.loop(1, ny)
-        def _(k):
+        for k in by_distance:
             pltpu.make_async_remote_copy(
                 src_ref=full.at[core, rows_of(gy)], dst_ref=full.at[core, rows_of(gy)],
                 send_sem=back_xy_send, recv_sem=back_xy_recv.at[k],
@@ -573,12 +590,11 @@
 
         share(gy)
 
-    @pl.loop(1, ny)
-    def _(k):
+    for k in reversed(by_distance):
         j = along_xy(ny - k)
 
         @pl.when(j < owners)
-        def _():
+        def _(j=j, k=k):
             pltpu.make_async_remote_copy(
                 src_ref=full.at[core, rows_of(j)], dst_ref=full.at[core, rows_of(j)],
                 send_sem=back_xy_send, recv_sem=back_xy_recv.at[k],
@@ -674,7 +690,8 @@
             vmem(field_in.shape, BF16), vmem(weight, BF16), vmem(weight, BF16), vmem(field_in.shape, BF16),
             dma((4,)), vmem(sums, F32), vmem(sums, F32),
             vmem(cells, F32), vmem(cells, F32), vmem(cells, F32),
-            vmem((Q, X * Y, 768), BF16), vmem((Q * Y, 768), BF16), vmem((2, Q, 24, 384), F32), vmem((X * Y, 128), F32),
+            vmem((Q, X * Y, 768), BF16), vmem((Q * Y, 768), BF16), vmem((2, Q, 24, 384), F32), vmem((2, Q, 24, 384), F32),
+            vmem((Q, X * Y, 128), F32), vmem((Q, X * Y, 128), F32),
             vmem((768, 384), BF16), vmem((768, 384), BF16), vmem((384, 768), BF16),
             vmem((256, Q * 128), BF16), vmem((256, Q * 128), BF16),
             vmem((Q, X * Y, 128), F32),

time: 46.7 us -> 45.1 us (0.966)
  Pallas kernels: 46 us -> 44.4 us
    pallas_call x1, Pallas kernels: 44.5 us -> 43 us  [shards(): pl.pallas_call(functools.partial(step, sizes), out_shape=(jax.ShapeDtypeS...]
where the time goes in v7:
time: 45.1 us; the launch traced here: 45 us
  Pallas kernels  44.4 us (98%)
  between operations  0.64 us (1%)
    pallas_call x1, Pallas kernels, shards(): pl.pallas_call(functools.partial(step, sizes), out_shape=(jax.ShapeDtypeS...  43 us
    pallas_call x1, Pallas kernels, shards(): pl.pallas_call(functools.partial(unpack, 1.0 / math.sqrt(total)), out_sha...  1.44 us

profile of v7, /device:TPU:1, one launch (start us, length us, event | category | flops | bytes accessed | tf_op | source)
XLA Modules:
  0.0 45.0 jit_solution(3274835305907969826)
XLA Ops:
  0.6 43.0 %shard_map.67 = (bf16[1,8,16,1024]{3,2,1,0:T(8,128)(2,1)S(1)}, bf16[2,960,128]{2,1,0:T(8,128)(2,1)S(1)}) custom-call(bf16[1,8,16,1024]{3,2,1,0:T(8,128)(2,1)} %field_hbm.1, bf16[27,64,64]{2,1,0:T(8,128)(2,1)} %bitcast.4, bf16[27,64,64]{2,1,0:T(8,128)(2,1)} %bitcast.5, bf16[1,8,16,1024]{3,2,1,0:T(8,128)(2,1)} %cotangent_hbm.1), custom_call_target="tpu_custom_call" | custom-call | tf_op jit(solution)/shard_map/pallas_call | solution.py:681
  43.6 1.4 %shard_map.68 = (bf16[1,8,16,1024]{3,2,1,0:T(8,128)(2,1)}, f32[27,64,64]{2,1,0:T(8,128)}, f32[27,64,64]{2,1,0:T(8,128)}) custom-call(bf16[1,8,16,1024]{3,2,1,0:T(8,128)(2,1)S(1)} %get-tuple-element.8.output_in, bf16[2,960,128]{2,1,0:T(8,128)(2,1)S(1)} %get-tuple-element.9.full), custom_call_target="tpu_custom_call" | custom-call | tf_op jit(solution)/shard_map/pallas_call | solution.py:718

commit v8 on v7

--- a/solution.py
+++ b/solution.py
@@ -189,17 +189,29 @@
     return [own.astype(BF16), mixed.astype(BF16)]
 
 
-def ring_x(ext, hidden_ext, banded, sided, gx, far):
+def slot_operand(ext, plane):
     low = low_lanes(SLOT)
-    total = jnp.zeros((Q * SLOT, 128), F32)
-    for dx, plane in enumerate((X + 2 * gx, far, FAR - (XE - 1) * gx)):
-        parts = []
-        for dy in range(3):
-            starts = [pl.multiple_of(row(q, plane, -8), 8) + dy - 1 for q in range(Q)]
-            parts += lanes_of([ext[pl.ds(start, SLOT), :] for start in starts], low)
-        total = total + jnp.dot(
-            jnp.concatenate(parts, axis=1), banded[:, dx * 128 : dx * 128 + 128], preferred_element_type=F32
-        )
+    parts = []
+    for dy in range(3):
+        starts = [pl.multiple_of(row(q, plane, -8), 8) + dy - 1 for q in range(Q)]
+        parts += lanes_of([ext[pl.ds(start, SLOT), :] for start in starts], low)
+    return jnp.concatenate(parts, axis=1)
+
+
+def ring_near(ext, banded, near_part, gx):
+    tap = pl.ds(pl.multiple_of(256 * gx, 128), 128)
+    near_part[...] = jnp.dot(
+        slot_operand(ext, X - (X - 1) * gx), banded[:, tap], preferred_element_type=F32
+    )
+
+
+def ring_far(ext, hidden_ext, banded, near_part, edge_part, sided, gx, far):
+    tap = pl.ds(pl.multiple_of((1 - gx) * 256, 128), 128)
+    both = jnp.concatenate([banded[:, tap], banded[:, 128:256]], axis=1)
+    result = jnp.dot(slot_operand(ext, far), both, preferred_element_type=F32)
+    edge_part[...] = result[:, 0:128]
+    total = near_part[...] + result[:, 128:256]
+    total = total + jnp.dot(slot_operand(ext, FAR), banded[:, tap], preferred_element_type=F32)
     hidden = silu(total)
     y = lax.broadcasted_iota(jnp.int32, (SLOT, 128), 0) - 8
     inside = ((y >= 0) & (y < Y)) | ((y == -1) & sided[0]) | ((y == Y) & sided[1])
@@ -208,7 +220,7 @@
         hidden_ext[pl.ds(pl.multiple_of(row(q, far, -8), 8), SLOT), :] = jnp.where(inside, part, jnp.zeros_like(part))
 
 
-def ring_y(ext, hidden_ext, banded, ring, sided):
+def ring_y(ext, hidden_ext, banded, ring, ring_pre, sided):
     low = low_lanes(PLANES)
     for side, y in ((0, -1), (1, Y)):
         parts = []
@@ -224,6 +236,7 @@
                 + ring[start + 1 : start + 1 + X, 128:256]
                 + ring[start + 2 : start + 2 + X, 256:384]
             )
+            ring_pre[side, pl.ds(q, X, stride=Q), :] = total
             hidden = silu(total)
             hidden_ext[pl.ds(row(q, 1, y), X, stride=SLOT), :] = jnp.where(
                 sided[side], hidden, jnp.zeros_like(hidden)
@@ -336,6 +349,7 @@
     banded_1, banded_2, banded_t, turned_c, turned_p, slope,
     send_xf, send_yf, send_cf, land_xf, land_yf, land_cf, corner_f,
     send_xc, send_yc, send_cc, land_xc, land_yc, land_cc, corner_c, ring,
+    ring_pre, near_part, edge_part,
     packed, gathered_xy, own_sum, pass_out, pass_in, gathered_z,
     halo_send, halo_recv, pass_send, pass_recv, xy_send, xy_recv, z_send, z_recv,
     back_xy_send, back_xy_recv, share_send, share_recv,
@@ -460,16 +474,23 @@
     conv_y(ext_c, banded_t, columns_c, True)
     for p in range(Q):
         conv_sum(shifted_c, columns_c, sums_c, p)
+    ring_y(ext_f, ext_h, banded_1, ring, ring_pre, sided)
+    ring_near(ext_f, banded_1, near_part, gx)
 
     arrive_x(0, ext_f)
-    add_plane(pre, conv_x(ext_f, thin, banded_1, False, gx, far), gx)
+    ring_far(ext_f, ext_h, banded_1, near_part, edge_part, sided, gx, far)
     edge = (X - 1) * (1 - gx)
     edge_rows = pl.ds(pl.multiple_of(edge * Y, Y), Y)
     for p in range(Q):
-        hidden, slope[p, edge_rows, :] = activate(pre[p, edge_rows, :])
+        added = edge_part[p * SLOT + 8 : p * SLOT + 8 + Y, :]
+        hidden, slope[p, edge_rows, :] = activate(pre[p, edge_rows, :] + added)
         ext_h[pl.ds(pl.multiple_of(row(p, edge + 1, 0), 8), Y), :] = hidden
-    ring_x(ext_f, ext_h, banded_1, sided, gx, far)
-    ring_y(ext_f, ext_h, banded_1, ring, sided)
+    for side, y in ((0, -1), (1, Y)):
+        added = edge_part[pl.ds(8 + y, Q, stride=SLOT), :]
+        hidden = silu(ring_pre[side, pl.ds(pl.multiple_of(edge * Q, Q), Q), :] + added)
+        ext_h[pl.ds(row(0, edge + 1, y), Q, stride=PLANES * SLOT), :] = jnp.where(
+            sided[side], hidden, jnp.zeros_like(hidden)
+        )
 
     owner = gy < owners
 
@@ -696,6 +717,7 @@
             vmem((256, Q * 128), BF16), vmem((256, Q * 128), BF16),
             vmem((Q, X * Y, 128), F32),
             *halo_buffers(2), *halo_buffers(1), vmem((Q * PLANES, 384), F32),
+            vmem((2, X * Q, 128), F32), vmem((Q * SLOT, 128), F32), vmem((Q * SLOT, 128), F32),
             vmem((2, rows, 128), BF16), vmem((2, ny, chunk, 128), BF16),
             vmem((chunk, 128), F32), vmem((chunk, 128), F32), vmem((chunk, 128), F32), vmem((nz, chunk, 128), BF16),
             dma((2, 5)), dma((2, 5)), dma, dma, dma((2,)), dma((2,)), dma, dma,

time: 45.1 us -> 44.9 us (level)
  no operation moved by 1% of the time
where the time goes in v8:
time: 44.9 us; the launch traced here: 44.8 us
  Pallas kernels  44.1 us (98%)
  between operations  0.64 us (1%)
    pallas_call x1, Pallas kernels, shards(): pl.pallas_call(functools.partial(step, sizes), out_shape=(jax.ShapeDtypeS...  42.7 us
    pallas_call x1, Pallas kernels, shards(): pl.pallas_call(functools.partial(unpack, 1.0 / math.sqrt(total)), out_sha...  1.44 us

profile of v8, /device:TPU:1, one launch (start us, length us, event | category | flops | bytes accessed | tf_op | source)
XLA Modules:
  0.0 44.8 jit_solution(3216972733607285442)
XLA Ops:
  0.6 42.7 %shard_map.67 = (bf16[1,8,16,1024]{3,2,1,0:T(8,128)(2,1)S(1)}, bf16[2,960,128]{2,1,0:T(8,128)(2,1)S(1)}) custom-call(bf16[1,8,16,1024]{3,2,1,0:T(8,128)(2,1)} %field_hbm.1, bf16[27,64,64]{2,1,0:T(8,128)(2,1)} %bitcast.4, bf16[27,64,64]{2,1,0:T(8,128)(2,1)} %bitcast.5, bf16[1,8,16,1024]{3,2,1,0:T(8,128)(2,1)} %cotangent_hbm.1), custom_call_target="tpu_custom_call" | custom-call | tf_op jit(solution)/shard_map/pallas_call | solution.py:702
  43.3 1.4 %shard_map.68 = (bf16[1,8,16,1024]{3,2,1,0:T(8,128)(2,1)}, f32[27,64,64]{2,1,0:T(8,128)}, f32[27,64,64]{2,1,0:T(8,128)}) custom-call(bf16[1,8,16,1024]{3,2,1,0:T(8,128)(2,1)S(1)} %get-tuple-element.8.output_in, bf16[2,960,128]{2,1,0:T(8,128)(2,1)S(1)} %get-tuple-element.9.full), custom_call_target="tpu_custom_call" | custom-call | tf_op jit(solution)/shard_map/pallas_call | solution.py:740

commit v9 on v8

--- a/solution.py
+++ b/solution.py
@@ -350,14 +350,14 @@
     send_xf, send_yf, send_cf, land_xf, land_yf, land_cf, corner_f,
     send_xc, send_yc, send_cc, land_xc, land_yc, land_cc, corner_c, ring,
     ring_pre, near_part, edge_part,
-    packed, gathered_xy, own_sum, pass_out, pass_in, gathered_z,
-    halo_send, halo_recv, pass_send, pass_recv, xy_send, xy_recv, z_send, z_recv,
+    packed, gathered_xy, gathered_z,
+    halo_send, halo_recv, xy_send, xy_recv, z_send, z_recv,
     back_xy_send, back_xy_recv, share_send, share_recv,
 ):
     nx, ny, ng = sizes
     zl = ng // 2
     nz = nx * zl
-    chunk = gathered_xy.shape[2]
+    chunk = gathered_xy.shape[1]
     owners = PACKED // chunk
     loads = [
         pltpu.make_async_copy(source, target, load_sems.at[number])
@@ -401,6 +401,10 @@
     def _(k):
         greet((gx, along_xy(k), grp))
 
+    @pl.loop(1, ny)
+    def _(k):
+        greet((gx, along_xy(k), grp + 1 - 2 * core))
+
     place = (gx, gy, grp)
     sided = (gy > 0, gy < ny - 1)
     far = (XE - 1) * (1 - gx)
@@ -417,7 +421,7 @@
     def dispatch(number, ext):
         take_edges(ext, *ends[number][:3], corners[number], gx)
         if number == 0:
-            pl.semaphore_wait(barrier, nz - 1 + ny - 1 + 3)
+            pl.semaphore_wait(barrier, nz - 1 + 2 * (ny - 1) + 3)
         for copy in halos[number]:
             copy.start()
 
@@ -500,12 +504,12 @@
                 if not pair * 192 < (j + 1) * chunk <= (pair + 1) * 192:
                     continue
 
-                @pl.when(gy != j)
+                @pl.when(jnp.logical_or(gy != j, core != g))
                 def _():
                     pltpu.make_async_remote_copy(
-                        src_ref=packed.at[g, pl.ds(j * chunk, chunk)], dst_ref=gathered_xy.at[g, gy],
-                        send_sem=xy_send.at[g], recv_sem=xy_recv.at[g],
-                        device_id=(gx, j, grp), device_id_type=MESH,
+                        src_ref=packed.at[g, pl.ds(j * chunk, chunk)], dst_ref=gathered_xy.at[core * ny + gy],
+                        send_sem=xy_send, recv_sem=xy_recv,
+                        device_id=(gx, j, grp + g - core), device_id_type=MESH,
                     ).start()
 
         return finished
@@ -528,45 +532,27 @@
     def rows_of(j):
         return pl.ds(pl.multiple_of(j * chunk, 16), chunk)
 
-    def several(g, count):
-        part = gathered_xy.at[g, pl.ds(0, count)]
+    def several(count):
+        part = gathered_xy.at[pl.ds(0, count)]
         return pltpu.make_async_remote_copy(
-            src_ref=part, dst_ref=part, send_sem=xy_send.at[g], recv_sem=xy_recv.at[g],
+            src_ref=part, dst_ref=part, send_sem=xy_send, recv_sem=xy_recv,
             device_id=me, device_id_type=MESH,
         )
 
-    pass_on = pltpu.make_async_remote_copy(
-        src_ref=pass_out, dst_ref=pass_in, send_sem=pass_send, recv_sem=pass_recv,
-        device_id=sibling, device_id_type=MESH,
-    )
-
-    for g in (1, 0):
-
-        @pl.when(owner)
-        def _():
-            several(g, ny - 1).wait_recv()
-            gathered_xy[g, gy] = packed[g, rows_of(gy), :]
-            total = gathered_xy[g, 0].astype(F32)
-            for k in range(1, ny):
-                total = total + gathered_xy[g, k].astype(F32)
-
-            @pl.when(core == 1 - g)
-            def _():
-                pass_out[...] = total
-                pass_on.start()
-
-            @pl.when(core == g)
-            def _():
-                own_sum[...] = total
-                pass_on.wait_recv()
-                gathered_z[z] = (own_sum[...] + pass_in[...]).astype(BF16)
-
-                for k in sorted(range(1, nz), key=lambda k: -min(k, nz - k)):
-                    pltpu.make_async_remote_copy(
-                        src_ref=gathered_z.at[z], dst_ref=gathered_z.at[z],
-                        send_sem=z_send, recv_sem=z_recv,
-                        device_id=z_device(along_z(k)), device_id_type=MESH,
-                    ).start()
+    @pl.when(owner)
+    def _():
+        several(2 * ny - 1).wait_recv()
+        gathered_xy[core * ny + gy] = packed[core, rows_of(gy), :]
+        total = gathered_xy[0].astype(F32)
+        for k in range(1, 2 * ny):
+            total = total + gathered_xy[k].astype(F32)
+        gathered_z[z] = total.astype(BF16)
+        for k in sorted(range(1, nz), key=lambda k: -min(k, nz - k)):
+            pltpu.make_async_remote_copy(
+                src_ref=gathered_z.at[z], dst_ref=gathered_z.at[z],
+                send_sem=z_send, recv_sem=z_recv,
+                device_id=z_device(along_z(k)), device_id_type=MESH,
+            ).start()
 
     def share(j):
         pltpu.make_async_remote_copy(
@@ -635,13 +621,11 @@
 
     @pl.when(owner)
     def _():
-        for g in range(2):
-            several(g, owners - 1).wait_send()
-        pass_on.wait_send()
+        several(2 * owners - 1).wait_send()
         z_all.wait_send()
+        part = gathered_xy.at[pl.ds(0, ny - 1)]
         pltpu.make_async_remote_copy(
-            src_ref=gathered_xy.at[0, pl.ds(0, ny - 1)], dst_ref=gathered_xy.at[0, pl.ds(0, ny - 1)],
-            send_sem=back_xy_send, recv_sem=share_recv,
+            src_ref=part, dst_ref=part, send_sem=back_xy_send, recv_sem=share_recv,
             device_id=me, device_id_type=MESH,
         ).wait_send()
 
@@ -649,8 +633,7 @@
 
         @pl.when(jnp.logical_not(owner))
         def _():
-            for g in range(2):
-                several(g, owners).wait_send()
+            several(2 * owners).wait_send()
 
     whole.wait_send()
 
@@ -718,9 +701,8 @@
             vmem((Q, X * Y, 128), F32),
             *halo_buffers(2), *halo_buffers(1), vmem((Q * PLANES, 384), F32),
             vmem((2, X * Q, 128), F32), vmem((Q * SLOT, 128), F32), vmem((Q * SLOT, 128), F32),
-            vmem((2, rows, 128), BF16), vmem((2, ny, chunk, 128), BF16),
-            vmem((chunk, 128), F32), vmem((chunk, 128), F32), vmem((chunk, 128), F32), vmem((nz, chunk, 128), BF16),
-            dma((2, 5)), dma((2, 5)), dma, dma, dma((2,)), dma((2,)), dma, dma,
+            vmem((2, rows, 128), BF16), vmem((2 * ny, chunk, 128), BF16), vmem((nz, chunk, 128), BF16),
+            dma((2, 5)), dma((2, 5)), dma, dma, dma, dma,
             dma, dma((ny,)), dma, dma,
         ],
         compiler_params=pltpu.CompilerParams(

time: 44.9 us -> 44.9 us (level)
  no operation moved by 1% of the time
where the time goes in v9:
time: 44.9 us; the launch traced here: 44.8 us
  Pallas kernels  44.2 us (98%)
  between operations  0.64 us (1%)
    pallas_call x1, Pallas kernels, shards(): pl.pallas_call(functools.partial(step, sizes), out_shape=(jax.ShapeDtypeS...  42.7 us
    pallas_call x1, Pallas kernels, shards(): pl.pallas_call(functools.partial(unpack, 1.0 / math.sqrt(total)), out_sha...  1.44 us

profile of v9, /device:TPU:1, one launch (start us, length us, event | category | flops | bytes accessed | tf_op | source)
XLA Modules:
  0.0 44.8 jit_solution(8349181500554042238)
XLA Ops:
  0.6 42.7 %shard_map.67 = (bf16[1,8,16,1024]{3,2,1,0:T(8,128)(2,1)S(1)}, bf16[2,960,128]{2,1,0:T(8,128)(2,1)S(1)}) custom-call(bf16[1,8,16,1024]{3,2,1,0:T(8,128)(2,1)} %field_hbm.1, bf16[27,64,64]{2,1,0:T(8,128)(2,1)} %bitcast.4, bf16[27,64,64]{2,1,0:T(8,128)(2,1)} %bitcast.5, bf16[1,8,16,1024]{3,2,1,0:T(8,128)(2,1)} %cotangent_hbm.1), custom_call_target="tpu_custom_call" | custom-call | tf_op jit(solution)/shard_map/pallas_call | solution.py:685
  43.4 1.4 %shard_map.68 = (bf16[1,8,16,1024]{3,2,1,0:T(8,128)(2,1)}, f32[27,64,64]{2,1,0:T(8,128)}, f32[27,64,64]{2,1,0:T(8,128)}) custom-call(bf16[1,8,16,1024]{3,2,1,0:T(8,128)(2,1)S(1)} %get-tuple-element.8.output_in, bf16[2,960,128]{2,1,0:T(8,128)(2,1)S(1)} %get-tuple-element.9.full), custom_call_target="tpu_custom_call" | custom-call | tf_op jit(solution)/shard_map/pallas_call | solution.py:722

commit v10 on v9

--- a/solution.py
+++ b/solution.py
@@ -397,12 +397,9 @@
         if k != zl:
             greet(z_device(along_z(k)))
 
-    @pl.loop(2, ny - 1)
-    def _(k):
+    for k in range(2, ny - 1):
         greet((gx, along_xy(k), grp))
-
-    @pl.loop(1, ny)
-    def _(k):
+    for k in range(1, ny):
         greet((gx, along_xy(k), grp + 1 - 2 * core))
 
     place = (gx, gy, grp)

time: 44.9 us -> 44.8 us (level)
  no operation moved by 1% of the time
where the time goes in v10:
time: 44.8 us; the launch traced here: 44.7 us
  Pallas kernels  44.1 us (98%)
  between operations  0.64 us (1%)
    pallas_call x1, Pallas kernels, shards(): pl.pallas_call(functools.partial(step, sizes), out_shape=(jax.ShapeDtypeS...  42.7 us
    pallas_call x1, Pallas kernels, shards(): pl.pallas_call(functools.partial(unpack, 1.0 / math.sqrt(total)), out_sha...  1.44 us

profile of v10, /device:TPU:1, one launch (start us, length us, event | category | flops | bytes accessed | tf_op | source)
XLA Modules:
  0.0 44.7 jit_solution(8951653151615915633)
XLA Ops:
  0.6 42.7 %shard_map.67 = (bf16[1,8,16,1024]{3,2,1,0:T(8,128)(2,1)S(1)}, bf16[2,960,128]{2,1,0:T(8,128)(2,1)S(1)}) custom-call(bf16[1,8,16,1024]{3,2,1,0:T(8,128)(2,1)} %field_hbm.1, bf16[27,64,64]{2,1,0:T(8,128)(2,1)} %bitcast.4, bf16[27,64,64]{2,1,0:T(8,128)(2,1)} %bitcast.5, bf16[1,8,16,1024]{3,2,1,0:T(8,128)(2,1)} %cotangent_hbm.1), custom_call_target="tpu_custom_call" | custom-call | tf_op jit(solution)/shard_map/pallas_call | solution.py:682
  43.3 1.4 %shard_map.68 = (bf16[1,8,16,1024]{3,2,1,0:T(8,128)(2,1)}, f32[27,64,64]{2,1,0:T(8,128)}, f32[27,64,64]{2,1,0:T(8,128)}) custom-call(bf16[1,8,16,1024]{3,2,1,0:T(8,128)(2,1)S(1)} %get-tuple-element.8.output_in, bf16[2,960,128]{2,1,0:T(8,128)(2,1)S(1)} %get-tuple-element.9.full), custom_call_target="tpu_custom_call" | custom-call | tf_op jit(solution)/shard_map/pallas_call | solution.py:719
